TPU v7x, 128 devices: a whole 4x4x4 slice. The times are simulated.
128 devices in a mesh: seq: 16 (over x, y), head: 8 (over z, core).
Axes of the slice: x: 4, y: 4, z: 4, core: 2. Of those that a mesh axis runs over, the one named last changes fastest.
Arguments:
- query: bfloat16 [16384, 7168], P(('seq', 'head')), may hold values from -16 to 16
- key: bfloat16 [16384, 7168], P(('seq', 'head')), may hold values from -16 to 16
- value: bfloat16 [16384, 7168], P(('seq', 'head')), may hold values from -8 to 8
- exponent: int32 [64], replicated, may hold values from 1 to 64, as said below
Outputs:
- attended: bfloat16 [16384, 7168], P(('seq', 'head'))
Inputs may be any that keep to these rules, and one draw needn't show every extreme that they name: Head h (counted from 0) has an exponent within 6 of h + 1; head 0 has 1 and the last head has 64.
All inputs are finite; a program needn't handle non-finite values.
Results may differ from a plain program's by a relative error of at most 0.0033.
Values may be sent and summed in bfloat16 or wider, within the bound.
A program may use at most 128 MiB of HBM per device.

v0:
```python
import jax
import jax.numpy as jnp
from jax import lax
from jax.sharding import PartitionSpec as P

BLOCK = 128
MIN_BAND = 16
MAX_BAND = 40


masked_score = -1e30


def passed_along(x, axis, by):
    length = lax.axis_size(axis)
    pairs = [(i, i + by) for i in range(length) if 0 <= i + by < length]
    return lax.ppermute(x, axis, pairs)


def attend_rows(
    query_block,
    keys_head,
    values_head,
    query_first,
    anchor,
    tile_low,
    tile_high,
    head_slope,
    head_band,
):
    block_rows, head_width = query_block.shape
    factor = head_width ** (-0.5)
    query_pos = query_first + jnp.arange(block_rows, dtype=jnp.int32)

    def tile_step(tile, state):
        running_max, weight_sum, accum = state
        tile_start = tile * block_rows
        key_tile = lax.dynamic_slice_in_dim(keys_head, tile_start, block_rows, 0)
        value_tile = lax.dynamic_slice_in_dim(values_head, tile_start, block_rows, 0)
        key_pos = anchor + tile_start + jnp.arange(block_rows, dtype=jnp.int32)
        distance = query_pos[:, None] - key_pos[None, :]
        scores = (
            lax.dot_general(
                query_block, key_tile, (((1,), (1,)), ((), ())), preferred_element_type=jnp.float32
            )
            * factor
        )
        scores = scores - head_slope * distance.astype(jnp.float32)
        live = (
            (key_pos[None, :] >= 0)
            & (distance >= 0)
            & (query_pos[:, None] // BLOCK - key_pos[None, :] // BLOCK < head_band)
        )
        scores = jnp.where(live, scores, masked_score)
        new_max = jnp.maximum(running_max, jnp.max(scores, axis=1, keepdims=True))
        weights = jnp.where(live, jnp.exp(scores - new_max), 0.0)
        shrink = jnp.exp(running_max - new_max)
        weight_sum = weight_sum * shrink + jnp.sum(weights, axis=1, keepdims=True)
        accum = accum * shrink + jnp.dot(
            weights.astype(jnp.bfloat16), value_tile, preferred_element_type=jnp.float32
        )
        return (new_max, weight_sum, accum)

    start_state = (
        jnp.full((block_rows, 1), masked_score, jnp.float32),
        jnp.zeros((block_rows, 1), jnp.float32),
        jnp.zeros((block_rows, head_width), jnp.float32),
    )
    final_state = lax.fori_loop(tile_low, tile_high + 1, tile_step, start_state)
    return (final_state[2] / final_state[1]).astype(jnp.bfloat16)


def on_device(query, key, value, exponent):
    token_rows, width_total = query.shape
    heads_total = exponent.shape[0]
    head_width = width_total // heads_total
    group_count = lax.axis_size("seq")
    slot_count = lax.axis_size("head")
    local_heads = heads_total // slot_count
    group_rows = token_rows * slot_count
    group_id = lax.axis_index("seq")
    slot_id = lax.axis_index("head")
    band_list = MIN_BAND + (exponent - 1) * (MAX_BAND - MIN_BAND) // (heads_total - 1)
    query_in, key_in, value_in = (query, key, value)
    head_ids = slot_id * local_heads + jnp.arange(local_heads, dtype=jnp.int32)
    local_exponent = jnp.take(exponent, head_ids)
    local_slopes = jnp.exp2(-12.0 * local_exponent.astype(jnp.float32) / heads_total)
    local_bands = jnp.take(band_list, head_ids)
    query_group, key_group, value_group = (
        lax.all_to_all(query_in, "head", split_axis=1, concat_axis=0, tiled=True),
        lax.all_to_all(key_in, "head", split_axis=1, concat_axis=0, tiled=True),
        lax.all_to_all(value_in, "head", split_axis=1, concat_axis=0, tiled=True),
    )
    local_width = query_group.shape[1]
    reach = min(((MAX_BAND - 1) * BLOCK + group_rows - 1) // group_rows, group_count - 1)
    key_pieces = []
    value_pieces = []
    for distance in range(1, reach + 1):
        moved_key, moved_value = passed_along((key_group, value_group), "seq", distance)
        key_pieces.insert(0, moved_key)
        value_pieces.insert(0, moved_value)
    keys_all = jnp.concatenate(key_pieces + [key_group], axis=0)
    values_all = jnp.concatenate(value_pieces + [value_group], axis=0)
    anchor = (group_id - reach) * group_rows
    query_rows = min(512, group_rows)

    def head_step(head_pos, out_buffer):
        column = head_pos * head_width
        query_head = lax.dynamic_slice_in_dim(query_group, column, head_width, 1)
        keys_head = lax.dynamic_slice_in_dim(keys_all, column, head_width, 1)
        values_head = lax.dynamic_slice_in_dim(values_all, column, head_width, 1)
        head_slope = local_slopes[head_pos]
        head_band = local_bands[head_pos]
        results = []
        for block_id in range(group_rows // query_rows):
            query_first = group_id * group_rows + block_id * query_rows
            first_block = query_first // BLOCK - (head_band - 1)
            lowest = jnp.maximum(jnp.maximum(first_block * BLOCK, 0) - anchor, 0)
            tile_low = lowest // query_rows
            tile_high = (reach * group_rows + block_id * query_rows) // query_rows
            query_block = query_head[block_id * query_rows : (block_id + 1) * query_rows]
            results.append(
                attend_rows(
                    query_block,
                    keys_head,
                    values_head,
                    query_first,
                    anchor,
                    tile_low,
                    tile_high,
                    head_slope,
                    head_band,
                )
            )
        head_result = jnp.concatenate(results, axis=0)
        return lax.dynamic_update_slice_in_dim(out_buffer, head_result, column, 1)

    attended_group = lax.fori_loop(
        0, local_heads, head_step, jnp.zeros((group_rows, local_width), jnp.bfloat16)
    )
    returned = lax.all_to_all(attended_group, "head", split_axis=0, concat_axis=1, tiled=True)
    return returned


def solution(mesh):
    return jax.shard_map(
        on_device,
        mesh=mesh,
        in_specs=(
            P(("seq", "head"), None),
            P(("seq", "head"), None),
            P(("seq", "head"), None),
            P(),
        ),
        out_specs=P(("seq", "head"), None),
        check_vma=False,
    )
```

profile of v0, /device:TPU:21, one launch (start us, length us, event | category | flops | bytes accessed | tf_op | source)
XLA Modules:
  0.0 1480.0 jit_solution(176938635701840083)
XLA Ops:
  1.8 29.6 %all_to_all.76 = bf16[128,8,896]{2,0,1:T(8,128)(2,1)} all-to-all(bf16[128,8,896]{2,0,1:T(8,128)(2,1)S(1)} %bitcast.99), channel_id=1, replica_groups=mesh['seq'=16,'head'=8] {'head'}, dimensions={1} | all-to-all | bytes 3670016 | tf_op jit(solution)/shard_map/all_to_all | solution.py:92
  40.3 4.8 all-to-all-start
  52.6 16.1 %all-to-all-done = bf16[128,8,896]{2,0,1:T(8,128)(2,1)S(1)} async-done(((bf16[128,8,896]{2,0,1:T(8,128)(2,1)}), bf16[128,8,896]{2,0,1:T(8,128)(2,1)S(1)}, u32[]{:S(2)}, u32[]{:S(2)}) %all-to-all-start) | async-done | bytes 1835040 | tf_op jit(solution)/shard_map/all_to_all | solution.py:91
  68.7 5.2 all-to-all-start.2
  78.6 35.6 %collective-permute-done.6 = bf16[1024,896]{1,0:T(8,128)(2,1)} collective-permute-done((bf16[1024,896]{1,0:T(8,128)(2,1)}, bf16[1024,896]{1,0:T(8,128)(2,1)}, u32[]{:S(2)}, u32[]{:S(2)}) %collective-permute-start.6) | collective-permute-done | bytes 1835040 | tf_op jit(solution)/shard_map/ppermute | solution.py:17
  117.0 73.5 %collective-permute-done.7 = bf16[1024,896]{1,0:T(8,128)(2,1)} collective-permute-done((bf16[1024,896]{1,0:T(8,128)(2,1)}, bf16[1024,896]{1,0:T(8,128)(2,1)}, u32[]{:S(2)}, u32[]{:S(2)}) %collective-permute-start.7) | collective-permute-done | bytes 1835040 | tf_op jit(solution)/shard_map/ppermute | solution.py:17
  190.5 5.0 collective-permute-start.2
  196.2 61.9 %collective-permute-done.8 = bf16[1024,896]{1,0:T(8,128)(2,1)} collective-permute-done((bf16[1024,896]{1,0:T(8,128)(2,1)}, bf16[1024,896]{1,0:T(8,128)(2,1)}, u32[]{:S(2)}, u32[]{:S(2)}) %collective-permute-start.8) | collective-permute-done | bytes 1835040 | tf_op jit(solution)/shard_map/ppermute | solution.py:17
  258.1 7.3 collective-permute-start.3
  278.8 19.4 %collective-permute-done = bf16[1024,896]{1,0:T(8,128)(2,1)} collective-permute-done((bf16[1024,896]{1,0:T(8,128)(2,1)S(1)}, bf16[1024,896]{1,0:T(8,128)(2,1)}, u32[]{:S(2)}, u32[]{:S(2)}) %collective-permute-start) | collective-permute-done | bytes 1835040 | tf_op jit(solution)/shard_map/ppermute | solution.py:17
  301.0 36.4 %collective-permute-done.1 = bf16[1024,896]{1,0:T(8,128)(2,1)} collective-permute-done((bf16[1024,896]{1,0:T(8,128)(2,1)S(1)}, bf16[1024,896]{1,0:T(8,128)(2,1)}, u32[]{:S(2)}, u32[]{:S(2)}) %collective-permute-start.1) | collective-permute-done | bytes 1835040 | tf_op jit(solution)/shard_map/ppermute | solution.py:17
  340.3 71.9 %collective-permute-done.2 = bf16[1024,896]{1,0:T(8,128)(2,1)} collective-permute-done((bf16[1024,896]{1,0:T(8,128)(2,1)S(1)}, bf16[1024,896]{1,0:T(8,128)(2,1)}, u32[]{:S(2)}, u32[]{:S(2)}) %collective-permute-start.2) | collective-permute-done | bytes 1835040 | tf_op jit(solution)/shard_map/ppermute | solution.py:17
  415.2 62.0 %collective-permute-done.3 = bf16[1024,896]{1,0:T(8,128)(2,1)} collective-permute-done((bf16[1024,896]{1,0:T(8,128)(2,1)S(1)}, bf16[1024,896]{1,0:T(8,128)(2,1)}, u32[]{:S(2)}, u32[]{:S(2)}) %collective-permute-start.3) | collective-permute-done | bytes 1835040 | tf_op jit(solution)/shard_map/ppermute | solution.py:17
  485.8 554.4 %while.112 = (s32[]{:T(128)}, bf16[1024,896]{0,1:T(8,128)(2,1)}, s32[8]{0:T(128)S(1)}, s32[]{:T(128)}, s32[]{:T(128)}, /*index=5*/bf16[6144,896]{1,0:T(8,128)(2,...) while((s32[]{:T(128)}, bf16[1024,896]{0,1:T(8,128)(2,1)}, ...), condition=%wide.region_9.11_spmd, body=%wide.region_0.10_spmd.sunk | while | flops 251566128 | bytes 15691133 | solution.py:138
  493.4 26.0 %while.114 = (s32[]{:T(128)}, f32[512,1]{0,1:T(1,128)S(1)}, f32[512,1]{0,1:T(1,128)S(1)}, f32[512,112]{0,1:T(8,128)S(1)}, s32[]{:T(128)}, /*index=5*/s32[]{:T(12...) while((s32[]{:T(128)}, f32[512,1]{0,1:T(1,128)S(1)}, ...), condition=%wide.region_4.5_spmd.clone.clone, body=%wide.region_1.4_spmd.clone.clone.sunk | while | flops 125438984 | bytes 4054259 | solution.py:69
  519.5 25.9 %while.113 = (s32[]{:T(128)}, f32[512,1]{0,1:T(1,128)S(1)}, f32[512,1]{0,1:T(1,128)S(1)}, f32[512,112]{0,1:T(8,128)S(1)}, s32[]{:T(128)}, /*index=5*/s32[]{:T(12...) while((s32[]{:T(128)}, f32[512,1]{0,1:T(1,128)S(1)}, ...), condition=%wide.region_8.9_spmd.clone.clone, body=%wide.region_5.8_spmd.clone.clone.sunk | while | flops 125438984 | bytes 4054259 | solution.py:69
  553.7 31.1 %while.114 = (s32[]{:T(128)}, f32[512,1]{0,1:T(1,128)S(1)}, f32[512,1]{0,1:T(1,128)S(1)}, f32[512,112]{0,1:T(8,128)S(1)}, s32[]{:T(128)}, /*index=5*/s32[]{:T(12...) while((s32[]{:T(128)}, f32[512,1]{0,1:T(1,128)S(1)}, ...), condition=%wide.region_4.5_spmd.clone.clone, body=%wide.region_1.4_spmd.clone.clone.sunk | while | flops 125438984 | bytes 4054259 | solution.py:69
  585.0 31.1 %while.113 = (s32[]{:T(128)}, f32[512,1]{0,1:T(1,128)S(1)}, f32[512,1]{0,1:T(1,128)S(1)}, f32[512,112]{0,1:T(8,128)S(1)}, s32[]{:T(128)}, /*index=5*/s32[]{:T(12...) while((s32[]{:T(128)}, f32[512,1]{0,1:T(1,128)S(1)}, ...), condition=%wide.region_8.9_spmd.clone.clone, body=%wide.region_5.8_spmd.clone.clone.sunk | while | flops 125438984 | bytes 4054259 | solution.py:69
  624.5 26.0 %while.114 = (s32[]{:T(128)}, f32[512,1]{0,1:T(1,128)S(1)}, f32[512,1]{0,1:T(1,128)S(1)}, f32[512,112]{0,1:T(8,128)S(1)}, s32[]{:T(128)}, /*index=5*/s32[]{:T(12...) while((s32[]{:T(128)}, f32[512,1]{0,1:T(1,128)S(1)}, ...), condition=%wide.region_4.5_spmd.clone.clone, body=%wide.region_1.4_spmd.clone.clone.sunk | while | flops 125438984 | bytes 4054259 | solution.py:69
  650.5 25.9 %while.113 = (s32[]{:T(128)}, f32[512,1]{0,1:T(1,128)S(1)}, f32[512,1]{0,1:T(1,128)S(1)}, f32[512,112]{0,1:T(8,128)S(1)}, s32[]{:T(128)}, /*index=5*/s32[]{:T(12...) while((s32[]{:T(128)}, f32[512,1]{0,1:T(1,128)S(1)}, ...), condition=%wide.region_8.9_spmd.clone.clone, body=%wide.region_5.8_spmd.clone.clone.sunk | while | flops 125438984 | bytes 4054259 | solution.py:69
  684.8 31.1 %while.114 = (s32[]{:T(128)}, f32[512,1]{0,1:T(1,128)S(1)}, f32[512,1]{0,1:T(1,128)S(1)}, f32[512,112]{0,1:T(8,128)S(1)}, s32[]{:T(128)}, /*index=5*/s32[]{:T(12...) while((s32[]{:T(128)}, f32[512,1]{0,1:T(1,128)S(1)}, ...), condition=%wide.region_4.5_spmd.clone.clone, body=%wide.region_1.4_spmd.clone.clone.sunk | while | flops 125438984 | bytes 4054259 | solution.py:69
  716.1 31.1 %while.113 = (s32[]{:T(128)}, f32[512,1]{0,1:T(1,128)S(1)}, f32[512,1]{0,1:T(1,128)S(1)}, f32[512,112]{0,1:T(8,128)S(1)}, s32[]{:T(128)}, /*index=5*/s32[]{:T(12...) while((s32[]{:T(128)}, f32[512,1]{0,1:T(1,128)S(1)}, ...), condition=%wide.region_8.9_spmd.clone.clone, body=%wide.region_5.8_spmd.clone.clone.sunk | while | flops 125438984 | bytes 4054259 | solution.py:69
  749.1 3.9 constant_dynamic-slice_fusion.5
  755.5 36.3 %while.114 = (s32[]{:T(128)}, f32[512,1]{0,1:T(1,128)S(1)}, f32[512,1]{0,1:T(1,128)S(1)}, f32[512,112]{0,1:T(8,128)S(1)}, s32[]{:T(128)}, /*index=5*/s32[]{:T(12...) while((s32[]{:T(128)}, f32[512,1]{0,1:T(1,128)S(1)}, ...), condition=%wide.region_4.5_spmd.clone.clone, body=%wide.region_1.4_spmd.clone.clone.sunk | while | flops 125438984 | bytes 4054259 | solution.py:69
  792.0 36.3 %while.113 = (s32[]{:T(128)}, f32[512,1]{0,1:T(1,128)S(1)}, f32[512,1]{0,1:T(1,128)S(1)}, f32[512,112]{0,1:T(8,128)S(1)}, s32[]{:T(128)}, /*index=5*/s32[]{:T(12...) while((s32[]{:T(128)}, f32[512,1]{0,1:T(1,128)S(1)}, ...), condition=%wide.region_8.9_spmd.clone.clone, body=%wide.region_5.8_spmd.clone.clone.sunk | while | flops 125438984 | bytes 4054259 | solution.py:69
  836.6 31.1 %while.114 = (s32[]{:T(128)}, f32[512,1]{0,1:T(1,128)S(1)}, f32[512,1]{0,1:T(1,128)S(1)}, f32[512,112]{0,1:T(8,128)S(1)}, s32[]{:T(128)}, /*index=5*/s32[]{:T(12...) while((s32[]{:T(128)}, f32[512,1]{0,1:T(1,128)S(1)}, ...), condition=%wide.region_4.5_spmd.clone.clone, body=%wide.region_1.4_spmd.clone.clone.sunk | while | flops 125438984 | bytes 4054259 | solution.py:69
  867.9 31.1 %while.113 = (s32[]{:T(128)}, f32[512,1]{0,1:T(1,128)S(1)}, f32[512,1]{0,1:T(1,128)S(1)}, f32[512,112]{0,1:T(8,128)S(1)}, s32[]{:T(128)}, /*index=5*/s32[]{:T(12...) while((s32[]{:T(128)}, f32[512,1]{0,1:T(1,128)S(1)}, ...), condition=%wide.region_8.9_spmd.clone.clone, body=%wide.region_5.8_spmd.clone.clone.sunk | while | flops 125438984 | bytes 4054259 | solution.py:69
  907.4 31.1 %while.114 = (s32[]{:T(128)}, f32[512,1]{0,1:T(1,128)S(1)}, f32[512,1]{0,1:T(1,128)S(1)}, f32[512,112]{0,1:T(8,128)S(1)}, s32[]{:T(128)}, /*index=5*/s32[]{:T(12...) while((s32[]{:T(128)}, f32[512,1]{0,1:T(1,128)S(1)}, ...), condition=%wide.region_4.5_spmd.clone.clone, body=%wide.region_1.4_spmd.clone.clone.sunk | while | flops 125438984 | bytes 4054259 | solution.py:69
  938.6 31.1 %while.113 = (s32[]{:T(128)}, f32[512,1]{0,1:T(1,128)S(1)}, f32[512,1]{0,1:T(1,128)S(1)}, f32[512,112]{0,1:T(8,128)S(1)}, s32[]{:T(128)}, /*index=5*/s32[]{:T(12...) while((s32[]{:T(128)}, f32[512,1]{0,1:T(1,128)S(1)}, ...), condition=%wide.region_8.9_spmd.clone.clone, body=%wide.region_5.8_spmd.clone.clone.sunk | while | flops 125438984 | bytes 4054259 | solution.py:69
  977.1 31.1 %while.114 = (s32[]{:T(128)}, f32[512,1]{0,1:T(1,128)S(1)}, f32[512,1]{0,1:T(1,128)S(1)}, f32[512,112]{0,1:T(8,128)S(1)}, s32[]{:T(128)}, /*index=5*/s32[]{:T(12...) while((s32[]{:T(128)}, f32[512,1]{0,1:T(1,128)S(1)}, ...), condition=%wide.region_4.5_spmd.clone.clone, body=%wide.region_1.4_spmd.clone.clone.sunk | while | flops 125438984 | bytes 4054259 | solution.py:69
  1008.3 31.1 %while.113 = (s32[]{:T(128)}, f32[512,1]{0,1:T(1,128)S(1)}, f32[512,1]{0,1:T(1,128)S(1)}, f32[512,112]{0,1:T(8,128)S(1)}, s32[]{:T(128)}, /*index=5*/s32[]{:T(12...) while((s32[]{:T(128)}, f32[512,1]{0,1:T(1,128)S(1)}, ...), condition=%wide.region_8.9_spmd.clone.clone, body=%wide.region_5.8_spmd.clone.clone.sunk | while | flops 125438984 | bytes 4054259 | solution.py:69
  1043.3 430.7 %all_to_all.77 = bf16[8,128,896]{2,1,0:T(8,128)(2,1)} all-to-all(bf16[8,128,896]{2,1,0:T(8,128)(2,1)S(1)} %bitcast.97), channel_id=1, replica_groups=mesh['seq'=16,'head'=8] {'head'}, dimensions={0} | all-to-all | bytes 3670016 | tf_op jit(solution)/shard_map/all_to_all | solution.py:141
  (1181 shorter events, 603.2 us)
Async XLA Ops:
  1.8 37.1 %copy-start.2 = (bf16[128,7168]{1,0:T(8,128)(2,1)S(1)}, bf16[128,7168]{1,0:T(8,128)(2,1)}, u32[]{:S(2)}) copy-start(bf16[128,7168]{1,0:T(8,128)(2,1)} %param.13) | copy-start | bytes 5505028
  31.4 43.7 %collective-permute-start.5 = (bf16[1024,896]{1,0:T(8,128)(2,1)}, bf16[1024,896]{1,0:T(8,128)(2,1)}, u32[]{:S(2)}, u32[]{:S(2)}) collective-permute-start(bf16[1024,896]{1,0:T(8,128)(2,1)} %bitcast.8), channel_id=1, source_target_pairs={{0,40},{8,48},{16,56},{24,64},{32,72},{40,80},{48,88},{56,96},{64,... | collective-permute-start | bytes 5505032 | tf_op jit(solution)/shard_map/ppermute | solution.py:17
  35.0 79.2 %collective-permute-start.6 = (bf16[1024,896]{1,0:T(8,128)(2,1)}, bf16[1024,896]{1,0:T(8,128)(2,1)}, u32[]{:S(2)}, u32[]{:S(2)}) collective-permute-start(bf16[1024,896]{1,0:T(8,128)(2,1)} %bitcast.8), channel_id=1, source_target_pairs={{0,32},{8,40},{16,48},{24,56},{32,64},{40,72},{48,80},{56,88},{64,... | collective-permute-start | bytes 5505032 | tf_op jit(solution)/shard_map/ppermute | solution.py:17
  36.9 153.6 %collective-permute-start.7 = (bf16[1024,896]{1,0:T(8,128)(2,1)}, bf16[1024,896]{1,0:T(8,128)(2,1)}, u32[]{:S(2)}, u32[]{:S(2)}) collective-permute-start(bf16[1024,896]{1,0:T(8,128)(2,1)} %bitcast.8), channel_id=1, source_target_pairs={{0,24},{8,32},{16,40},{24,48},{32,56},{40,64},{48,72},{56,80},{64,... | collective-permute-start | bytes 5505032 | tf_op jit(solution)/shard_map/ppermute | solution.py:17
  40.3 28.4 %all-to-all-start = ((bf16[128,8,896]{2,0,1:T(8,128)(2,1)}), bf16[128,8,896]{2,0,1:T(8,128)(2,1)S(1)}, u32[]{:S(2)}, u32[]{:S(2)}) async-start(bf16[128,8,896]{2,0,1:T(8,128)(2,1)} %bitcast.96), calls=%async_computation | async-start | bytes 3670016 | tf_op jit(solution)/shard_map/all_to_all | solution.py:91
  45.1 213.0 %collective-permute-start.8 = (bf16[1024,896]{1,0:T(8,128)(2,1)}, bf16[1024,896]{1,0:T(8,128)(2,1)}, u32[]{:S(2)}, u32[]{:S(2)}) collective-permute-start(bf16[1024,896]{1,0:T(8,128)(2,1)} %bitcast.8), channel_id=1, source_target_pairs={{0,16},{8,24},{16,32},{24,40},{32,48},{40,56},{48,64},{56,72},{64,... | collective-permute-start | bytes 5505032 | tf_op jit(solution)/shard_map/ppermute | solution.py:17
  47.5 217.9 %collective-permute-start.9 = (bf16[1024,896]{1,0:T(8,128)(2,1)}, bf16[1024,896]{1,0:T(8,128)(2,1)}, u32[]{:S(2)}, u32[]{:S(2)}) collective-permute-start(bf16[1024,896]{1,0:T(8,128)(2,1)} %bitcast.8), channel_id=1, source_target_pairs={{0,8},{8,16},{16,24},{24,32},{32,40},{40,48},{48,56},{56,64},{64,7... | collective-permute-start | bytes 5505032 | tf_op jit(solution)/shard_map/ppermute | solution.py:17
  68.7 48.3 %copy-start = (s32[64]{0:T(128)S(1)}, s32[64]{0:T(128)}, u32[]{:S(2)}) copy-start(s32[64]{0:T(128)} %param.15) | copy-start | bytes 772
  68.7 415.7 %all-to-all-start.2 = ((bf16[128,8,896]{2,0,1:T(8,128)(2,1)}), bf16[128,8,896]{2,0,1:T(8,128)(2,1)}, u32[]{:S(2)}, u32[]{:S(2)}) async-start(bf16[128,8,896]{2,0,1:T(8,128)(2,1)} %bitcast.95), calls=%async_computation.2 | async-start | bytes 3670016 | tf_op jit(solution)/shard_map/all_to_all | solution.py:90
  75.1 223.0 %collective-permute-start = (bf16[1024,896]{1,0:T(8,128)(2,1)S(1)}, bf16[1024,896]{1,0:T(8,128)(2,1)}, u32[]{:S(2)}, u32[]{:S(2)}) collective-permute-start(bf16[1024,896]{1,0:T(8,128)(2,1)S(1)} %bitcast.89), channel_id=1, source_target_pairs={{0,40},{8,48},{16,56},{24,64},{32,72},{40,80},{48,88},{56,96},{64,... | collective-permute-start | bytes 5505032 | tf_op jit(solution)/shard_map/ppermute | solution.py:17
  114.2 223.3 %collective-permute-start.1 = (bf16[1024,896]{1,0:T(8,128)(2,1)S(1)}, bf16[1024,896]{1,0:T(8,128)(2,1)}, u32[]{:S(2)}, u32[]{:S(2)}) collective-permute-start(bf16[1024,896]{1,0:T(8,128)(2,1)S(1)} %bitcast.90), channel_id=1, source_target_pairs={{0,32},{8,40},{16,48},{24,56},{32,64},{40,72},{48,80},{56,88},{64,... | collective-permute-start | bytes 5505032 | tf_op jit(solution)/shard_map/ppermute | solution.py:17
  190.5 221.7 %collective-permute-start.2 = (bf16[1024,896]{1,0:T(8,128)(2,1)S(1)}, bf16[1024,896]{1,0:T(8,128)(2,1)}, u32[]{:S(2)}, u32[]{:S(2)}) collective-permute-start(bf16[1024,896]{1,0:T(8,128)(2,1)S(1)} %bitcast.91), channel_id=1, source_target_pairs={{0,24},{8,32},{16,40},{24,48},{32,56},{40,64},{48,72},{56,80},{64,... | collective-permute-start | bytes 5505032 | tf_op jit(solution)/shard_map/ppermute | solution.py:17
  258.1 219.0 %collective-permute-start.3 = (bf16[1024,896]{1,0:T(8,128)(2,1)S(1)}, bf16[1024,896]{1,0:T(8,128)(2,1)}, u32[]{:S(2)}, u32[]{:S(2)}) collective-permute-start(bf16[1024,896]{1,0:T(8,128)(2,1)S(1)} %bitcast.92), channel_id=1, source_target_pairs={{0,16},{8,24},{16,32},{24,40},{32,48},{40,56},{48,64},{56,72},{64,... | collective-permute-start | bytes 5505032 | tf_op jit(solution)/shard_map/ppermute | solution.py:17
  265.5 214.6 %collective-permute-start.4 = (bf16[1024,896]{1,0:T(8,128)(2,1)S(1)}, bf16[1024,896]{1,0:T(8,128)(2,1)}, u32[]{:S(2)}, u32[]{:S(2)}) collective-permute-start(bf16[1024,896]{1,0:T(8,128)(2,1)S(1)} %bitcast.93), channel_id=1, source_target_pairs={{0,8},{8,16},{16,24},{24,32},{32,40},{40,48},{48,56},{56,64},{64,7... | collective-permute-start | bytes 5505032 | tf_op jit(solution)/shard_map/ppermute | solution.py:17
  278.7 201.3 %copy-start.1 = (bf16[6144,896]{1,0:T(8,128)(2,1)}, bf16[6144,896]{1,0:T(8,128)(2,1)S(1)}, u32[]{:S(2)}) copy-start(bf16[6144,896]{1,0:T(8,128)(2,1)S(1)} %constant_dynamic-update-slice_fusion.6) | copy-start | bytes 33030148
where the time goes:
time: 1490 us; the launch traced here: 1480 us
  blocking collectives  460 us (31%)
  waiting for transfers between devices  378 us (25%)
  matrix products  369 us (25%)
  other arithmetic  117 us (8%)
  local copies, waits for them, and re-layouts  99.9 us (7%)
  starting transfers between devices  42.2 us (3%)
    all_to_all x1, blocking collectives, on_device(): lax.all_to_all(attended_group, 'head', split_axis=0, concat_axis=1, tiled...  431 us
    ppermute x10, waiting for transfers between devices, passed_along(): return lax.ppermute(x, axis, pairs)  362 us
    dot_general x94, matrix products, tile_step(): lax.dot_general(query_block, key_tile, (((1,), (1,)), ((), ())), preferre...  249 us
    dot_general x94, matrix products, tile_step(): jnp.dot(weights.astype(jnp.bfloat16), value_tile, preferred_element_type=...  120 us
    reduce_sum x94, other arithmetic, tile_step(): weight_sum = weight_sum * shrink + jnp.sum(weights, axis=1, keepdims=True)  102 us
    ppermute x10, starting transfers between devices, passed_along(): return lax.ppermute(x, axis, pairs)  32.2 us
    dynamic_slice x8, local copies, waits for them, and re-layouts, head_step(): values_head = lax.dynamic_slice_in_dim(values_all, column, head_width, 1)  30.5 us
  transfers between devices with their start and end apart: 12, of which 9 were waited for; matrix products, arithmetic and copies ran while one was open for 2% of the time, Pallas kernels for 0%

commit v1 on v0

v1 whole, which is shorter than its diff:
```python
import functools

import jax
import jax.numpy as jnp
from jax import lax
from jax.experimental import pallas as pl
from jax.experimental.pallas import tpu as pltpu
from jax.sharding import PartitionSpec as P

BLOCK = 128
MIN_BAND = 16
MAX_BAND = 40
HEADS = 64
HS = 112
D = HEADS * HS
PLANE = 32
HALO = 40
MESH = pl.DeviceIdType.MESH
LOG2E = 1.4426950408889634


def coords():
    seq = lax.axis_index("seq")
    head = lax.axis_index("head")
    x = seq // 4
    p = (seq % 4) * 8 + head
    return x, p


def device_of(x, p):
    return (x * 4 + p // 8, p % 8)


def most_band(slot, p):
    if slot == 0:
        return MIN_BAND + (p + 6) * 24 // 63
    return MIN_BAND + (69 - p) * 24 // 63


def head_of(slot, p):
    return p if slot == 0 else HEADS - 1 - p


def head_rows(slot, p):
    return pl.ds(pl.multiple_of(head_of(slot, p) * HS, 16), HS)


def enter(x, p):
    barrier = pltpu.get_barrier_semaphore()

    def greet(d, carry):
        pl.semaphore_signal(
            barrier, inc=1, device_id=device_of(x, (p + d) % PLANE), device_id_type=MESH
        )
        return carry

    lax.fori_loop(1, PLANE, greet, 0)
    for d in range(1, 4):
        pl.semaphore_signal(barrier, inc=1, device_id=device_of((x + d) % 4, p), device_id_type=MESH)
    pl.semaphore_wait(barrier, PLANE - 1 + 3)


def dispatch_kernel(
    q_ref, k_ref, v_ref, group, halo, turned, send, recv, halo_send, halo_recv, far_send, own
):
    x, p = coords()
    eye = (
        lax.broadcasted_iota(jnp.int32, (BLOCK, BLOCK), 0)
        == lax.broadcasted_iota(jnp.int32, (BLOCK, BLOCK), 1)
    ).astype(jnp.bfloat16)

    def turn(step, carry):
        for part in range(4):
            at = pl.multiple_of((step * 4 + part) * BLOCK, BLOCK)
            for c, ref in enumerate((q_ref, k_ref, v_ref)):
                tile = ref[:, pl.ds(at, BLOCK)]
                turned[c, pl.ds(at, BLOCK), :] = lax.dot_general(
                    eye, tile, (((1,), (1,)), ((), ())), preferred_element_type=jnp.float32
                ).astype(jnp.bfloat16)
        return carry

    lax.fori_loop(0, D // BLOCK // 4, turn, 0)
    enter(x, p)

    def to_peer(d, slot):
        peer = (p + d) % PLANE
        return pltpu.make_async_remote_copy(
            src_ref=turned.at[:, head_rows(slot, peer), :],
            dst_ref=group.at[p, slot],
            send_sem=send.at[d, slot],
            recv_sem=recv.at[p, slot],
            device_id=device_of(x, peer),
            device_id_type=MESH,
        )

    def from_peer(j, slot):
        return pltpu.make_async_remote_copy(
            src_ref=turned.at[:, pl.ds(0, HS), :],
            dst_ref=group.at[j, slot],
            send_sem=send.at[0, slot],
            recv_sem=recv.at[j, slot],
            device_id=device_of(x, (p + 1) % PLANE),
            device_id_type=MESH,
        )

    def near(j, slot):
        return pltpu.make_async_remote_copy(
            src_ref=group.at[j, slot, pl.ds(1, 2)],
            dst_ref=halo.at[8 + j, slot],
            send_sem=halo_send.at[j, slot],
            recv_sem=halo_recv.at[8 + j, slot],
            device_id=device_of((x + 1) % 4, p),
            device_id_type=MESH,
        )

    def far(j):
        return pltpu.make_async_remote_copy(
            src_ref=group.at[j, 1, pl.ds(1, 2)],
            dst_ref=halo.at[j - 24, 1],
            send_sem=far_send.at[j - 24],
            recv_sem=halo_recv.at[j - 24, 1],
            device_id=device_of((x + 2) % 4, p),
            device_id_type=MESH,
        )

    def start_all(d, carry):
        for slot in range(2):
            to_peer(d, slot).start()
        return carry

    lax.fori_loop(1, PLANE, start_all, 0)
    own_copies = [
        pltpu.make_async_copy(
            turned.at[:, head_rows(slot, p), :], group.at[p, slot], own.at[slot]
        )
        for slot in range(2)
    ]
    for copy in own_copies:
        copy.start()

    def near_needed(j, slot):
        return (x < 3) & (j >= 33 - most_band(slot, p))

    def far_needed(j):
        return (x < 2) & (j >= 25) & (j >= 65 - most_band(1, p))

    def forward(j, slot):
        @pl.when(near_needed(j, slot))
        def _():
            near(j, slot).start()

        if slot == 1:

            @pl.when(far_needed(j))
            def _():
                far(j).start()

    for slot, copy in enumerate(own_copies):
        copy.wait()
        forward(p, slot)

    def take(d, carry):
        j = (p + PLANE - d) % PLANE
        for slot in range(2):
            from_peer(j, slot).wait_recv()
            forward(j, slot)
        return carry

    lax.fori_loop(1, PLANE, take, 0)

    def finish(d, carry):
        for slot in range(2):
            @pl.when(d > 0)
            def _():
                to_peer(d, slot).wait_send()

            @pl.when(near_needed(d, slot))
            def _():
                near(d, slot).wait_send()

            @pl.when((x > 0) & (d >= 33 - most_band(slot, p)))
            def _():
                near(d, slot).wait_recv()

        @pl.when(far_needed(d))
        def _():
            far(d).wait_send()

        @pl.when((x > 1) & (d >= 25) & (d >= 65 - most_band(1, p)))
        def _():
            far(d).wait_recv()

        return carry

    lax.fori_loop(0, PLANE, finish, 0)


def dispatch(query, key, value):
    return pl.pallas_call(
        dispatch_kernel,
        out_shape=(
            jax.ShapeDtypeStruct((PLANE, 2, 3, HS, BLOCK), jnp.bfloat16),
            jax.ShapeDtypeStruct((HALO, 2, 2, HS, BLOCK), jnp.bfloat16),
        ),
        in_specs=[pl.BlockSpec(memory_space=pltpu.VMEM)] * 3,
        out_specs=(pl.BlockSpec(memory_space=pl.ANY), pl.BlockSpec(memory_space=pl.ANY)),
        scratch_shapes=[
            pltpu.VMEM((3, D, BLOCK), jnp.bfloat16),
            pltpu.SemaphoreType.DMA((PLANE, 2)),
            pltpu.SemaphoreType.DMA((PLANE, 2)),
            pltpu.SemaphoreType.DMA((PLANE, 2)),
            pltpu.SemaphoreType.DMA((HALO, 2)),
            pltpu.SemaphoreType.DMA((8,)),
            pltpu.SemaphoreType.DMA((2,)),
        ],
        compiler_params=pltpu.CompilerParams(
            collective_id=0, has_side_effects=True, vmem_limit_bytes=40 << 20
        ),
        name="dispatch",
    )(query, key, value)


def attend_kernel(
    band_ref, where_ref, slope_ref, group, halo, out, keys, values, weight_rows, acc_a, acc_b
):
    slot = pl.program_id(0)
    step = pl.program_id(1)
    x = where_ref[0]
    band = band_ref[slot]
    factor = HS ** (-0.5)
    scale = factor * LOG2E

    @pl.when(step == 0)
    def _():
        eye = (
            lax.broadcasted_iota(jnp.int32, (BLOCK, BLOCK), 0)
            == lax.broadcasted_iota(jnp.int32, (BLOCK, BLOCK), 1)
        ).astype(jnp.bfloat16)
        row = lax.broadcasted_iota(jnp.int32, (16, BLOCK), 0)
        token = lax.broadcasted_iota(jnp.int32, (16, BLOCK), 1).astype(jnp.float32)
        ones = jnp.ones((16, BLOCK), jnp.bfloat16)

        def put(index, key_t, value_t):
            block = (index - HALO).astype(jnp.float32)
            extra = jnp.where(row < 3, block, jnp.where(row < 6, token, 0.0)).astype(jnp.bfloat16)
            whole = jnp.concatenate([key_t, extra], axis=0)
            at = pl.multiple_of(index * BLOCK, BLOCK)
            keys[pl.ds(at, BLOCK), :] = lax.dot_general(
                eye, whole, (((1,), (1,)), ((), ())), preferred_element_type=jnp.float32
            ).astype(jnp.bfloat16)
            values[:, pl.ds(at, BLOCK)] = jnp.concatenate([value_t, ones], axis=0)

        def put_halo(index, carry):
            live = (index - HALO >= -PLANE * x) & (index - HALO > -band)

            @pl.when(live)
            def _():
                put(index, halo[index, 0, 0], halo[index, 0, 1])

            @pl.when(jnp.logical_not(live))
            def _():
                nothing = jnp.zeros((HS, BLOCK), jnp.bfloat16)
                put(index, nothing, nothing)

            return carry

        lax.fori_loop(0, HALO, put_halo, 0)

        def put_group(index, carry):
            put(index + HALO, group[index, 0, 1], group[index, 0, 2])
            return carry

        lax.fori_loop(0, PLANE, put_group, 0)

        slope = slope_ref[0:1, :] * (BLOCK / factor)
        high = slope.astype(jnp.bfloat16).astype(jnp.float32)
        middle = (slope - high).astype(jnp.bfloat16).astype(jnp.float32)
        low = (slope - high - middle).astype(jnp.bfloat16).astype(jnp.float32)
        kind = row % 3
        parts = jnp.where(kind == 0, high, jnp.where(kind == 1, middle, low))
        parts = jnp.where(row < 3, parts, jnp.where(row < 6, parts * (1.0 / BLOCK), 0.0))
        weight_rows[...] = jnp.concatenate([parts, parts], axis=1).astype(jnp.bfloat16)

    def query_tile(first):
        pair = jnp.concatenate([group[first, 0, 0], group[first + 1, 0, 0]], axis=1)
        return jnp.concatenate([pair, weight_rows[...]], axis=0)

    def scores(first_block, count, query):
        at = pl.multiple_of((first_block + HALO) * BLOCK, BLOCK)
        return jnp.dot(
            keys[pl.ds(at, count * BLOCK), :], query, preferred_element_type=jnp.float32
        )

    def mix(first_block, count, weight):
        at = pl.multiple_of((first_block + HALO) * BLOCK, BLOCK)
        return jnp.dot(
            values[:, pl.ds(at, count * BLOCK)],
            weight.astype(jnp.bfloat16),
            preferred_element_type=jnp.float32,
        )

    firsts = (step * 4, step * 4 + 2)
    queries = [query_tile(first) for first in firsts]
    accs = (acc_a, acc_b)
    wide = 2 * BLOCK
    causal = lax.broadcasted_iota(jnp.int32, (wide, wide), 0) <= lax.broadcasted_iota(
        jnp.int32, (wide, wide), 1
    )
    tops = []
    for first, query, acc in zip(firsts, queries, accs):
        s = jnp.where(causal, scores(first, 2, query), -1e30)
        top = jnp.max(s, axis=0, keepdims=True)
        acc[...] = mix(first, 2, jnp.exp2((s - top) * scale))
        tops.append(top)

    def go(first, query, acc, top, start, live):
        s = scores(start, 4, query)
        if live is not None:
            s = jnp.where(live, s, -1e30)
        new = jnp.maximum(top, jnp.max(s, axis=0, keepdims=True))
        weight = jnp.exp2((s - new) * scale)
        shrink = jnp.exp2((top - new) * scale)
        acc[...] = acc[...] * shrink + mix(start, 4, weight)
        return new

    full = jnp.minimum(band - 2, step * 4 + PLANE * x) // 4

    def middle_step(n, tops):
        return tuple(
            go(first, query, acc, top, first - 4 * n - 4, None)
            for first, query, acc, top in zip(firsts, queries, accs, tops)
        )

    tops = lax.fori_loop(0, full, middle_step, tuple(tops))
    key_block = lax.broadcasted_iota(jnp.int32, (4 * BLOCK, wide), 0) // BLOCK
    query_block = lax.broadcasted_iota(jnp.int32, (4 * BLOCK, wide), 1) // BLOCK
    for part, (first, query, acc, top) in enumerate(zip(firsts, queries, accs, tops)):
        start = first - 4 * full - 4
        live = (key_block + start > query_block + (first - band)) & (
            key_block + start >= -PLANE * x
        )
        go(first, query, acc, top, start, live)
        result = (acc[0:HS, :] / acc[HS : HS + 1, :]).astype(jnp.bfloat16)
        out[2 * part, 0] = result[:, :BLOCK]
        out[2 * part + 1, 0] = result[:, BLOCK:]


def attend(bands, where, slopes, group, halo):
    return pl.pallas_call(
        attend_kernel,
        out_shape=jax.ShapeDtypeStruct((PLANE, 2, HS, BLOCK), jnp.bfloat16),
        grid_spec=pltpu.PrefetchScalarGridSpec(
            num_scalar_prefetch=2,
            grid=(2, PLANE // 4),
            in_specs=[
                pl.BlockSpec((None, 8, BLOCK), lambda i, j, *_: (i, 0, 0)),
                pl.BlockSpec((PLANE, 1, 3, HS, BLOCK), lambda i, j, *_: (0, i, 0, 0, 0)),
                pl.BlockSpec((HALO, 1, 2, HS, BLOCK), lambda i, j, *_: (0, i, 0, 0, 0)),
            ],
            out_specs=pl.BlockSpec((4, 1, HS, BLOCK), lambda i, j, *_: (j, i, 0, 0)),
            scratch_shapes=[
                pltpu.VMEM(((HALO + PLANE) * BLOCK, BLOCK), jnp.bfloat16),
                pltpu.VMEM((BLOCK, (HALO + PLANE) * BLOCK), jnp.bfloat16),
                pltpu.VMEM((16, 2 * BLOCK), jnp.bfloat16),
                pltpu.VMEM((BLOCK, 2 * BLOCK), jnp.float32),
                pltpu.VMEM((BLOCK, 2 * BLOCK), jnp.float32),
            ],
        ),
        compiler_params=pltpu.CompilerParams(
            dimension_semantics=("arbitrary", "arbitrary"), vmem_limit_bytes=50 << 20
        ),
        name="attend",
    )(bands, where, slopes, group, halo)


def combine_kernel(mixed, out, back, send, recv, own):
    x, p = coords()
    enter(x, p)

    def to_peer(d, slot):
        peer = (p + d) % PLANE
        return pltpu.make_async_remote_copy(
            src_ref=mixed.at[peer, slot],
            dst_ref=back.at[head_rows(slot, p), :],
            send_sem=send.at[d, slot],
            recv_sem=recv.at[p, slot],
            device_id=device_of(x, peer),
            device_id_type=MESH,
        )

    def from_peer(j, slot):
        return pltpu.make_async_remote_copy(
            src_ref=mixed.at[0, slot],
            dst_ref=back.at[head_rows(slot, j), :],
            send_sem=send.at[0, slot],
            recv_sem=recv.at[j, slot],
            device_id=device_of(x, (p + 1) % PLANE),
            device_id_type=MESH,
        )

    def start_all(d, carry):
        for slot in range(2):
            to_peer(d, slot).start()
        return carry

    lax.fori_loop(1, PLANE, start_all, 0)
    for slot in range(2):
        copy = pltpu.make_async_copy(
            mixed.at[p, slot], back.at[head_rows(slot, p), :], own.at[slot]
        )
        copy.start()
        copy.wait()

    def finish(d, carry):
        j = (p + PLANE - d) % PLANE
        for slot in range(2):
            from_peer(j, slot).wait_recv()
            to_peer(d, slot).wait_send()
        return carry

    lax.fori_loop(1, PLANE, finish, 0)
    eye = (
        lax.broadcasted_iota(jnp.int32, (BLOCK, BLOCK), 0)
        == lax.broadcasted_iota(jnp.int32, (BLOCK, BLOCK), 1)
    ).astype(jnp.bfloat16)

    def turn(step, carry):
        for part in range(4):
            at = pl.multiple_of((step * 4 + part) * BLOCK, BLOCK)
            out[:, pl.ds(at, BLOCK)] = lax.dot_general(
                eye, back[pl.ds(at, BLOCK), :], (((1,), (1,)), ((), ())),
                preferred_element_type=jnp.float32,
            ).astype(jnp.bfloat16)
        return carry

    lax.fori_loop(0, D // BLOCK // 4, turn, 0)


def combine(mixed):
    return pl.pallas_call(
        combine_kernel,
        out_shape=jax.ShapeDtypeStruct((BLOCK, D), jnp.bfloat16),
        in_specs=[pl.BlockSpec(memory_space=pltpu.VMEM)],
        out_specs=pl.BlockSpec(memory_space=pltpu.VMEM),
        scratch_shapes=[
            pltpu.VMEM((D, BLOCK), jnp.bfloat16),
            pltpu.SemaphoreType.DMA((PLANE, 2)),
            pltpu.SemaphoreType.DMA((PLANE, 2)),
            pltpu.SemaphoreType.DMA((2,)),
        ],
        compiler_params=pltpu.CompilerParams(
            collective_id=1, has_side_effects=True, vmem_limit_bytes=40 << 20
        ),
        name="combine",
    )(mixed)


def on_device(query, key, value, exponent):
    x, p = coords()
    heads = jnp.stack([p, HEADS - 1 - p])
    local = jnp.take(exponent, heads)
    bands = MIN_BAND + (local - 1) * (MAX_BAND - MIN_BAND) // (HEADS - 1)
    slopes = jnp.exp2(-12.0 * local.astype(jnp.float32) / HEADS)
    slopes = jnp.broadcast_to(slopes[:, None, None], (2, 8, BLOCK))
    group, halo = dispatch(query, key, value)
    mixed = attend(bands, x[None], slopes, group, halo)
    return combine(mixed)


def solution(mesh):
    return jax.shard_map(
        on_device,
        mesh=mesh,
        in_specs=(
            P(("seq", "head"), None),
            P(("seq", "head"), None),
            P(("seq", "head"), None),
            P(),
        ),
        out_specs=P(("seq", "head"), None),
        check_vma=False,
    )
```

time: 1490 us -> 362 us (0.24)
  blocking collectives: 460 us -> 0 us
  waiting for transfers between devices: 378 us -> 0 us
  matrix products: 369 us -> 0 us
  Pallas kernels: 0 us -> 347 us
  other arithmetic: 117 us -> 0.19 us
  local copies, waits for them, and re-layouts: 99.9 us -> 9.14 us
  starting transfers between devices: 42.2 us -> 0 us
    all_to_all x2 -> x0, blocking collectives: 460 us -> none  [the longest x1 431 us: on_device(): lax.all_to_all(attended_group, 'head', split_axis=0, concat_axis=1, tiled...]
    dot_general x188 -> x0, matrix products: 369 us -> none  [the longest x94 249 us: tile_step(): lax.dot_general(query_block, key_tile, (((1,), (1,)), ((), ())), preferre...]
    ppermute x10 -> x0, waiting for transfers between devices: 362 us -> none  [passed_along(): return lax.ppermute(x, axis, pairs)]
    pallas_call x0 -> x3, Pallas kernels: none -> 347 us  [the longest x1 155 us: dispatch(): pl.pallas_call(dispatch_kernel, out_shape=(jax.ShapeDtypeStruct((PLANE, 2...]
    reduce_sum x94 -> x0, other arithmetic: 102 us -> none  [tile_step(): weight_sum = weight_sum * shrink + jnp.sum(weights, axis=1, keepdims=True)]
    dynamic_slice x24 -> x0, local copies, waits for them, and re-layouts: 39.3 us -> none  [the longest x8 30.5 us: head_step(): values_head = lax.dynamic_slice_in_dim(values_all, column, head_width, 1)]
    ppermute x10 -> x0, starting transfers between devices: 32.2 us -> none  [passed_along(): return lax.ppermute(x, axis, pairs)]
    all_to_all x2 -> x0, waiting for transfers between devices: 16.1 us -> none  [the longest x1 16.1 us: on_device(): lax.all_to_all(key_in, 'head', split_axis=1, concat_axis=0, tiled=True)]
  transfers between devices with their start and end apart: 12 -> 0, of which waited for: 9 -> 0; matrix products, arithmetic and copies ran while one was open for 2% -> 0% of each run, Pallas kernels for 0% -> 0%
where the time goes in v1:
time: 362 us; the launch traced here: 356 us
  Pallas kernels  347 us (96%)
  local copies, waits for them, and re-layouts  9.14 us (3%)
    pallas_call x1, Pallas kernels, dispatch(): pl.pallas_call(dispatch_kernel, out_shape=(jax.ShapeDtypeStruct((PLANE, 2...  155 us
    pallas_call x1, Pallas kernels, attend(): pl.pallas_call(attend_kernel, out_shape=jax.ShapeDtypeStruct((PLANE, 2, H...  141 us
    pallas_call x1, Pallas kernels, combine(): pl.pallas_call(combine_kernel, out_shape=jax.ShapeDtypeStruct((BLOCK, D),...  50.9 us
    unnamed x11, local copies, waits for them, and re-layouts  8.43 us

profile of v1, /device:TPU:21, one launch (start us, length us, event | category | flops | bytes accessed | tf_op | source)
XLA Modules:
  0.0 356.3 jit_solution(10657547085037473298)
XLA Ops:
  0.0 0.0 copy-start
  0.0 0.1 fusion
  0.1 0.6 copy-done
  0.7 0.6 gather_fusion
  1.3 0.1 multiply_exponential_fusion
  1.4 0.1 broadcast_in_dim.12.slope_ref
  1.5 0.0 copy-start.2
  1.5 1.5 copy-done.2
  3.0 0.0 copy-start.3
  3.0 1.5 copy-done.3
  4.5 0.0 copy-start.4
  4.5 1.5 copy-done.4
  6.0 155.3 %dispatch.1 = (bf16[32,2,3,112,128]{4,3,2,1,0:T(8,128)(2,1)}, bf16[40,2,2,112,128]{4,3,2,1,0:T(8,128)(2,1)S(1)}) custom-call(bf16[128,7168]{1,0:T(8,128)(2,1)S(1)} %copy-done.2, bf16[128,7168]{1,0:T(8,128)(2,1)S(1)} %copy-done.3, bf16[128,7168]{1,0:T(8,128)(2,1)S(1)} %copy-done.4), custom_call_target="tpu_custom_call" | custom-call | tf_op jit(solution)/shard_map/dispatch/pallas_call | solution.py:199
  161.3 0.0 copy-start.1
  161.3 2.1 copy-done.1
  163.4 140.7 %attend.1.mixed = bf16[32,2,112,128]{3,2,1,0:T(8,128)(2,1)S(1)} custom-call(s32[2]{0:T(128)S(1)} %fusion.1.band_ref, s32[1]{0:T(128)} %bitcast.5.where_ref, f32[2,8,128]{2,1,0:T(8,128)S(1)} %broadcast_in_dim.12.slope_ref, bf16[32,2,3,112,128]{4,3,2,1,0:T(8,128)(2,1)} %get-tuple-element.7.group, bf16[40,2,2,112,128]{4,3,2,1,0:T(8,128)(2,1)} %copy-done.1), custom_call_target="tpu_custom_call" | custom-call | tf_op jit(solution)/shard_map/attend/pallas_call | solution.py:349
  304.1 50.9 %combine.1 = bf16[128,7168]{1,0:T(8,128)(2,1)S(1)} custom-call(bf16[32,2,112,128]{3,2,1,0:T(8,128)(2,1)S(1)} %attend.1.mixed), custom_call_target="tpu_custom_call" | custom-call | tf_op jit(solution)/shard_map/combine/pallas_call | solution.py:440
  355.0 1.2 copy.6
  (2 shorter events, 0.0 us)
Async XLA Ops:
  0.0 0.7 copy-start
  1.5 1.5 copy-start.2
  3.0 1.5 copy-start.3
  4.5 1.5 copy-start.4
  161.3 2.1 copy-start.1

commit v2 on v1

--- a/solution.py
+++ b/solution.py
@@ -17,6 +17,7 @@
 HALO = 40
 MESH = pl.DeviceIdType.MESH
 LOG2E = 1.4426950408889634
+PARTS = (pl.ds(1, 2), pl.ds(0, 1))
 
 
 def coords():
@@ -82,23 +83,23 @@
     lax.fori_loop(0, D // BLOCK // 4, turn, 0)
     enter(x, p)
 
-    def to_peer(d, slot):
+    def to_peer(d, slot, part):
         peer = (p + d) % PLANE
         return pltpu.make_async_remote_copy(
-            src_ref=turned.at[:, head_rows(slot, peer), :],
-            dst_ref=group.at[p, slot],
-            send_sem=send.at[d, slot],
-            recv_sem=recv.at[p, slot],
+            src_ref=turned.at[PARTS[part], head_rows(slot, peer), :],
+            dst_ref=group.at[p, slot, PARTS[part]],
+            send_sem=send.at[d, slot, part],
+            recv_sem=recv.at[p, slot, part],
             device_id=device_of(x, peer),
             device_id_type=MESH,
         )
 
-    def from_peer(j, slot):
+    def from_peer(j, slot, part):
         return pltpu.make_async_remote_copy(
-            src_ref=turned.at[:, pl.ds(0, HS), :],
-            dst_ref=group.at[j, slot],
-            send_sem=send.at[0, slot],
-            recv_sem=recv.at[j, slot],
+            src_ref=turned.at[PARTS[part], pl.ds(0, HS), :],
+            dst_ref=group.at[j, slot, PARTS[part]],
+            send_sem=send.at[0, slot, part],
+            recv_sem=recv.at[j, slot, part],
             device_id=device_of(x, (p + 1) % PLANE),
             device_id_type=MESH,
         )
@@ -123,12 +124,15 @@
             device_id_type=MESH,
         )
 
-    def start_all(d, carry):
-        for slot in range(2):
-            to_peer(d, slot).start()
-        return carry
-
-    lax.fori_loop(1, PLANE, start_all, 0)
+    for part in range(2):
+
+        def start_all(d, carry):
+            for slot in range(2):
+                to_peer(d, slot, part).start()
+            return carry
+
+        lax.fori_loop(1, PLANE, start_all, 0)
+
     own_copies = [
         pltpu.make_async_copy(
             turned.at[:, head_rows(slot, p), :], group.at[p, slot], own.at[slot]
@@ -162,7 +166,7 @@
     def take(d, carry):
         j = (p + PLANE - d) % PLANE
         for slot in range(2):
-            from_peer(j, slot).wait_recv()
+            from_peer(j, slot, 0).wait_recv()
             forward(j, slot)
         return carry
 
@@ -172,7 +176,9 @@
         for slot in range(2):
             @pl.when(d > 0)
             def _():
-                to_peer(d, slot).wait_send()
+                from_peer((p + d) % PLANE, slot, 1).wait_recv()
+                for part in range(2):
+                    to_peer(d, slot, part).wait_send()
 
             @pl.when(near_needed(d, slot))
             def _():
@@ -206,8 +212,8 @@
         out_specs=(pl.BlockSpec(memory_space=pl.ANY), pl.BlockSpec(memory_space=pl.ANY)),
         scratch_shapes=[
             pltpu.VMEM((3, D, BLOCK), jnp.bfloat16),
-            pltpu.SemaphoreType.DMA((PLANE, 2)),
-            pltpu.SemaphoreType.DMA((PLANE, 2)),
+            pltpu.SemaphoreType.DMA((PLANE, 2, 2)),
+            pltpu.SemaphoreType.DMA((PLANE, 2, 2)),
             pltpu.SemaphoreType.DMA((PLANE, 2)),
             pltpu.SemaphoreType.DMA((HALO, 2)),
             pltpu.SemaphoreType.DMA((8,)),
@@ -220,129 +226,156 @@
     )(query, key, value)
 
 
+PAD = 48
+TILE = 4
+ROWS = TILE * BLOCK
+CHAINS = PLANE // TILE
+TAIL = 6
+
+
+def unit():
+    return (
+        lax.broadcasted_iota(jnp.int32, (BLOCK, BLOCK), 0)
+        == lax.broadcasted_iota(jnp.int32, (BLOCK, BLOCK), 1)
+    ).astype(jnp.bfloat16)
+
+
+def flip(x):
+    size = x.shape[1]
+    one = (
+        lax.broadcasted_iota(jnp.int32, (size, size), 0)
+        == lax.broadcasted_iota(jnp.int32, (size, size), 1)
+    ).astype(jnp.bfloat16)
+    return lax.dot_general(
+        one, x, (((1,), (1,)), ((), ())), preferred_element_type=jnp.float32
+    ).astype(jnp.bfloat16)
+
+
 def attend_kernel(
-    band_ref, where_ref, slope_ref, group, halo, out, keys, values, weight_rows, acc_a, acc_b
+    band_ref, where_ref, slope_ref, group, halo, out, keys, values, queries, acc_ref
 ):
-    slot = pl.program_id(0)
-    step = pl.program_id(1)
     x = where_ref[0]
-    band = band_ref[slot]
+    band = band_ref[pl.program_id(0)]
     factor = HS ** (-0.5)
     scale = factor * LOG2E
-
-    @pl.when(step == 0)
-    def _():
-        eye = (
-            lax.broadcasted_iota(jnp.int32, (BLOCK, BLOCK), 0)
-            == lax.broadcasted_iota(jnp.int32, (BLOCK, BLOCK), 1)
-        ).astype(jnp.bfloat16)
-        row = lax.broadcasted_iota(jnp.int32, (16, BLOCK), 0)
-        token = lax.broadcasted_iota(jnp.int32, (16, BLOCK), 1).astype(jnp.float32)
-        ones = jnp.ones((16, BLOCK), jnp.bfloat16)
-
-        def put(index, key_t, value_t):
-            block = (index - HALO).astype(jnp.float32)
-            extra = jnp.where(row < 3, block, jnp.where(row < 6, token, 0.0)).astype(jnp.bfloat16)
-            whole = jnp.concatenate([key_t, extra], axis=0)
-            at = pl.multiple_of(index * BLOCK, BLOCK)
-            keys[pl.ds(at, BLOCK), :] = lax.dot_general(
-                eye, whole, (((1,), (1,)), ((), ())), preferred_element_type=jnp.float32
-            ).astype(jnp.bfloat16)
-            values[:, pl.ds(at, BLOCK)] = jnp.concatenate([value_t, ones], axis=0)
-
-        def put_halo(index, carry):
+    row = lax.broadcasted_iota(jnp.int32, (16, BLOCK), 0)
+    token = lax.broadcasted_iota(jnp.int32, (16, BLOCK), 1).astype(jnp.float32)
+    ones = jnp.ones((16, BLOCK), jnp.bfloat16)
+    nothing = jnp.zeros((HS, BLOCK), jnp.bfloat16)
+
+    def put(index, key_t, value_t, dead):
+        block = (index - PAD).astype(jnp.float32)
+        extra = jnp.where(
+            row < 3, block, jnp.where(row < 6, token, jnp.where(row < 7, dead, 0.0))
+        )
+        at = pl.multiple_of(index * BLOCK, BLOCK)
+        keys[:, pl.ds(at, BLOCK)] = jnp.concatenate([key_t, extra.astype(jnp.bfloat16)], axis=0)
+        values[:, pl.ds(at, BLOCK)] = jnp.concatenate([value_t, ones], axis=0)
+
+    def put_pad(index, carry):
+        put(index, nothing, nothing, 1.0)
+        return carry
+
+    lax.fori_loop(0, PAD - HALO, put_pad, 0)
+
+    def put_halo(step, carry):
+        for part in range(4):
+            index = step * 4 + part
             live = (index - HALO >= -PLANE * x) & (index - HALO > -band)
 
             @pl.when(live)
             def _():
-                put(index, halo[index, 0, 0], halo[index, 0, 1])
+                put(index + PAD - HALO, halo[index, 0, 0], halo[index, 0, 1], 0.0)
 
             @pl.when(jnp.logical_not(live))
             def _():
-                nothing = jnp.zeros((HS, BLOCK), jnp.bfloat16)
-                put(index, nothing, nothing)
-
-            return carry
-
-        lax.fori_loop(0, HALO, put_halo, 0)
-
-        def put_group(index, carry):
-            put(index + HALO, group[index, 0, 1], group[index, 0, 2])
-            return carry
-
-        lax.fori_loop(0, PLANE, put_group, 0)
-
-        slope = slope_ref[0:1, :] * (BLOCK / factor)
-        high = slope.astype(jnp.bfloat16).astype(jnp.float32)
-        middle = (slope - high).astype(jnp.bfloat16).astype(jnp.float32)
-        low = (slope - high - middle).astype(jnp.bfloat16).astype(jnp.float32)
-        kind = row % 3
-        parts = jnp.where(kind == 0, high, jnp.where(kind == 1, middle, low))
-        parts = jnp.where(row < 3, parts, jnp.where(row < 6, parts * (1.0 / BLOCK), 0.0))
-        weight_rows[...] = jnp.concatenate([parts, parts], axis=1).astype(jnp.bfloat16)
-
-    def query_tile(first):
-        pair = jnp.concatenate([group[first, 0, 0], group[first + 1, 0, 0]], axis=1)
-        return jnp.concatenate([pair, weight_rows[...]], axis=0)
-
-    def scores(first_block, count, query):
-        at = pl.multiple_of((first_block + HALO) * BLOCK, BLOCK)
+                put(index + PAD - HALO, nothing, nothing, 1.0)
+
+        return carry
+
+    lax.fori_loop(0, HALO // 4, put_halo, 0)
+    slope = slope_ref[0:1, :] * (BLOCK / factor)
+    high = slope.astype(jnp.bfloat16).astype(jnp.float32)
+    middle = (slope - high).astype(jnp.bfloat16).astype(jnp.float32)
+    low = (slope - high - middle).astype(jnp.bfloat16).astype(jnp.float32)
+    kind = row % 3
+    parts = jnp.where(kind == 0, high, jnp.where(kind == 1, middle, low))
+    parts = jnp.where(
+        row < 3, parts, jnp.where(row < 6, parts * (1.0 / BLOCK), jnp.where(row < 7, -1e30, 0.0))
+    ).astype(jnp.bfloat16)
+
+    def put_group(step, carry):
+        for part in range(8):
+            index = step * 8 + part
+            put(index + PAD, group[index, 0, 1], group[index, 0, 2], 0.0)
+            queries[pl.ds(pl.multiple_of(index * BLOCK, BLOCK), BLOCK), :] = flip(
+                jnp.concatenate([group[index, 0, 0], parts], axis=0)
+            )
+        return carry
+
+    lax.fori_loop(0, PLANE // 8, put_group, 0)
+
+    def scores(chain, first, count):
+        at = pl.multiple_of((first + PAD) * BLOCK, BLOCK)
         return jnp.dot(
-            keys[pl.ds(at, count * BLOCK), :], query, preferred_element_type=jnp.float32
-        )
-
-    def mix(first_block, count, weight):
-        at = pl.multiple_of((first_block + HALO) * BLOCK, BLOCK)
-        return jnp.dot(
+            queries[chain * ROWS : (chain + 1) * ROWS, :],
+            keys[:, pl.ds(at, count * BLOCK)],
+            preferred_element_type=jnp.float32,
+        )
+
+    def mix(first, count, weight):
+        at = pl.multiple_of((first + PAD) * BLOCK, BLOCK)
+        return lax.dot_general(
+            weight.astype(jnp.bfloat16),
             values[:, pl.ds(at, count * BLOCK)],
-            weight.astype(jnp.bfloat16),
+            (((1,), (1,)), ((), ())),
             preferred_element_type=jnp.float32,
         )
 
-    firsts = (step * 4, step * 4 + 2)
-    queries = [query_tile(first) for first in firsts]
-    accs = (acc_a, acc_b)
-    wide = 2 * BLOCK
-    causal = lax.broadcasted_iota(jnp.int32, (wide, wide), 0) <= lax.broadcasted_iota(
-        jnp.int32, (wide, wide), 1
+    causal = lax.broadcasted_iota(jnp.int32, (ROWS, ROWS), 1) <= lax.broadcasted_iota(
+        jnp.int32, (ROWS, ROWS), 0
     )
-    tops = []
-    for first, query, acc in zip(firsts, queries, accs):
-        s = jnp.where(causal, scores(first, 2, query), -1e30)
-        top = jnp.max(s, axis=0, keepdims=True)
-        acc[...] = mix(first, 2, jnp.exp2((s - top) * scale))
-        tops.append(top)
-
-    def go(first, query, acc, top, start, live):
-        s = scores(start, 4, query)
-        if live is not None:
-            s = jnp.where(live, s, -1e30)
-        new = jnp.maximum(top, jnp.max(s, axis=0, keepdims=True))
-        weight = jnp.exp2((s - new) * scale)
-        shrink = jnp.exp2((top - new) * scale)
-        acc[...] = acc[...] * shrink + mix(start, 4, weight)
-        return new
-
-    full = jnp.minimum(band - 2, step * 4 + PLANE * x) // 4
-
-    def middle_step(n, tops):
-        return tuple(
-            go(first, query, acc, top, first - 4 * n - 4, None)
-            for first, query, acc, top in zip(firsts, queries, accs, tops)
-        )
-
-    tops = lax.fori_loop(0, full, middle_step, tuple(tops))
-    key_block = lax.broadcasted_iota(jnp.int32, (4 * BLOCK, wide), 0) // BLOCK
-    query_block = lax.broadcasted_iota(jnp.int32, (4 * BLOCK, wide), 1) // BLOCK
-    for part, (first, query, acc, top) in enumerate(zip(firsts, queries, accs, tops)):
-        start = first - 4 * full - 4
-        live = (key_block + start > query_block + (first - band)) & (
-            key_block + start >= -PLANE * x
-        )
-        go(first, query, acc, top, start, live)
-        result = (acc[0:HS, :] / acc[HS : HS + 1, :]).astype(jnp.bfloat16)
-        out[2 * part, 0] = result[:, :BLOCK]
-        out[2 * part + 1, 0] = result[:, BLOCK:]
+    starting = []
+    for c in range(CHAINS):
+        s = jnp.where(causal, scores(c, c * TILE, TILE), -1e30)
+        top = jnp.max(s, axis=1, keepdims=True)
+        acc_ref[c] = mix(c * TILE, TILE, jnp.exp2((s - top) * scale))
+        starting.append(top)
+
+    def sweep(tops, offset, count, live):
+        starts = [c * TILE + offset for c in range(CHAINS)]
+
+        def tile(c):
+            s = scores(c, starts[c], count)
+            if live is not None:
+                s = jnp.where(live, s, -1e30)
+            return s, jnp.maximum(tops[c], jnp.max(s, axis=1, keepdims=True))
+
+        after = []
+        ready = tile(0)
+        for c in range(CHAINS):
+            s, new = ready
+            if c + 1 < CHAINS:
+                ready = tile(c + 1)
+            weight = jnp.exp2((s - new) * scale)
+            acc_ref[c] = acc_ref[c] * jnp.exp2((tops[c] - new) * scale) + mix(
+                starts[c], count, weight
+            )
+            after.append(new)
+        return tuple(after)
+
+    full = (band - TILE) // TILE
+    tops = lax.fori_loop(
+        0, full, lambda n, tops: sweep(tops, -TILE * n - TILE, TILE, None), tuple(starting)
+    )
+    key_block = lax.broadcasted_iota(jnp.int32, (ROWS, TAIL * BLOCK), 1) // BLOCK
+    query_block = lax.broadcasted_iota(jnp.int32, (ROWS, TAIL * BLOCK), 0) // BLOCK
+    offset = -TILE * full - TAIL
+    sweep(tops, offset, TAIL, key_block + offset > query_block - band)
+    for c in range(CHAINS):
+        result = (acc_ref[c, :, 0:HS] / acc_ref[c, :, HS : HS + 1]).astype(jnp.bfloat16)
+        for b in range(TILE):
+            out[c * TILE + b, 0] = flip(result[b * BLOCK : (b + 1) * BLOCK])
 
 
 def attend(bands, where, slopes, group, halo):
@@ -351,23 +384,22 @@
         out_shape=jax.ShapeDtypeStruct((PLANE, 2, HS, BLOCK), jnp.bfloat16),
         grid_spec=pltpu.PrefetchScalarGridSpec(
             num_scalar_prefetch=2,
-            grid=(2, PLANE // 4),
+            grid=(2,),
             in_specs=[
-                pl.BlockSpec((None, 8, BLOCK), lambda i, j, *_: (i, 0, 0)),
-                pl.BlockSpec((PLANE, 1, 3, HS, BLOCK), lambda i, j, *_: (0, i, 0, 0, 0)),
-                pl.BlockSpec((HALO, 1, 2, HS, BLOCK), lambda i, j, *_: (0, i, 0, 0, 0)),
+                pl.BlockSpec((None, 8, BLOCK), lambda i, *_: (i, 0, 0)),
+                pl.BlockSpec((PLANE, 1, 3, HS, BLOCK), lambda i, *_: (0, i, 0, 0, 0)),
+                pl.BlockSpec((HALO, 1, 2, HS, BLOCK), lambda i, *_: (0, i, 0, 0, 0)),
             ],
-            out_specs=pl.BlockSpec((4, 1, HS, BLOCK), lambda i, j, *_: (j, i, 0, 0)),
+            out_specs=pl.BlockSpec((PLANE, 1, HS, BLOCK), lambda i, *_: (0, i, 0, 0)),
             scratch_shapes=[
-                pltpu.VMEM(((HALO + PLANE) * BLOCK, BLOCK), jnp.bfloat16),
-                pltpu.VMEM((BLOCK, (HALO + PLANE) * BLOCK), jnp.bfloat16),
-                pltpu.VMEM((16, 2 * BLOCK), jnp.bfloat16),
-                pltpu.VMEM((BLOCK, 2 * BLOCK), jnp.float32),
-                pltpu.VMEM((BLOCK, 2 * BLOCK), jnp.float32),
+                pltpu.VMEM((BLOCK, (PAD + PLANE) * BLOCK), jnp.bfloat16),
+                pltpu.VMEM((BLOCK, (PAD + PLANE) * BLOCK), jnp.bfloat16),
+                pltpu.VMEM((PLANE * BLOCK, BLOCK), jnp.bfloat16),
+                pltpu.VMEM((CHAINS, ROWS, BLOCK), jnp.float32),
             ],
         ),
         compiler_params=pltpu.CompilerParams(
-            dimension_semantics=("arbitrary", "arbitrary"), vmem_limit_bytes=50 << 20
+            dimension_semantics=("arbitrary",), vmem_limit_bytes=56 << 20
         ),
         name="attend",
     )(bands, where, slopes, group, halo)

time: 362 us -> 247 us (0.68)
  the two profiles are of different devices: /device:TPU:21 before, /device:TPU:115 now
where the time goes in v2:
time: 247 us
  Pallas kernels  235 us (95%)
  local copies, waits for them, and re-layouts  11.2 us (5%)
    pallas_call x1, Pallas kernels, dispatch(): pl.pallas_call(dispatch_kernel, out_shape=(jax.ShapeDtypeStruct((PLANE, 2...  122 us
    pallas_call x1, Pallas kernels, attend(): pl.pallas_call(attend_kernel, out_shape=jax.ShapeDtypeStruct((PLANE, 2, H...  57.1 us
    pallas_call x1, Pallas kernels, combine(): pl.pallas_call(combine_kernel, out_shape=jax.ShapeDtypeStruct((BLOCK, D),...  56.4 us
    unnamed x13, local copies, waits for them, and re-layouts  9.92 us

profile of v2, /device:TPU:115, one launch (start us, length us, event | category | flops | bytes accessed | tf_op | source)
XLA Modules:
  0.0 247.2 jit_solution(7889512887591137583)
XLA Ops:
  0.0 0.0 copy-start
  0.0 0.1 fusion
  0.1 0.6 copy-done
  0.7 0.6 gather_fusion
  1.3 0.1 multiply_exponential_fusion
  1.4 0.5 fusion.1.band_ref
  1.9 0.7 broadcast_in_dim.12.slope_ref
  2.6 0.0 copy-start.3
  2.6 1.5 copy-done.3
  4.1 0.0 copy-start.4
  4.1 1.5 copy-done.4
  5.6 0.0 copy-start.5
  5.6 1.5 copy-done.5
  7.1 121.7 %dispatch.1 = (bf16[32,2,3,112,128]{4,3,2,1,0:T(8,128)(2,1)}, bf16[40,2,2,112,128]{4,3,2,1,0:T(8,128)(2,1)S(1)}) custom-call(bf16[128,7168]{1,0:T(8,128)(2,1)S(1)} %copy-done.3, bf16[128,7168]{1,0:T(8,128)(2,1)S(1)} %copy-done.4, bf16[128,7168]{1,0:T(8,128)(2,1)S(1)} %copy-done.5), custom_call_target="tpu_custom_call" | custom-call | tf_op jit(solution)/shard_map/dispatch/pallas_call | solution.py:205
  128.8 0.0 copy-start.2
  128.8 2.1 copy-done.2
  131.0 57.1 %attend.1.mixed = bf16[32,2,112,128]{3,2,1,0:T(8,128)(2,1)} custom-call(s32[2]{0:T(128)} %fusion.1.band_ref, s32[1]{0:T(128)} %bitcast.5.where_ref, f32[2,8,128]{2,1,0:T(8,128)} %broadcast_in_dim.12.slope_ref, bf16[32,2,3,112,128]{4,3,2,1,0:T(8,128)(2,1)} %get-tuple-element.7.group, bf16[40,2,2,112,128]{4,3,2,1,0:T(8,128)(2,1)} %copy-done.2), custom_call_target="tpu_custom_call" | custom-call | tf_op jit(solution)/shard_map/attend/pallas_call | solution.py:382
  188.0 0.0 copy-start.1
  188.0 1.5 copy-done.1
  189.5 56.4 %combine.1 = bf16[128,7168]{1,0:T(8,128)(2,1)S(1)} custom-call(bf16[32,2,112,128]{3,2,1,0:T(8,128)(2,1)S(1)} %copy-done.1), custom_call_target="tpu_custom_call" | custom-call | tf_op jit(solution)/shard_map/combine/pallas_call | solution.py:472
  246.0 1.2 copy.6
  (1 shorter events, 0.0 us)
Async XLA Ops:
  0.0 0.7 copy-start
  2.6 1.5 copy-start.3
  4.1 1.5 copy-start.4
  5.6 1.5 copy-start.5
  128.8 2.1 copy-start.2
  188.0 1.5 copy-start.1

commit v3 on v0

v3 whole, which is shorter than its diff:
```python
import jax
import jax.numpy as jnp
from jax import lax
from jax.experimental import pallas as pl
from jax.experimental.pallas import tpu as pltpu
from jax.sharding import PartitionSpec as P

BLOCK = 128
MIN_BAND = 16
MAX_BAND = 40
HEADS = 64
HS = 112
D = HEADS * HS
HALF = D // 2
PLANE = 32
PAD = 48
TILE = 4
ROWS = TILE * BLOCK
CHAINS = PLANE // TILE
MESH = pl.DeviceIdType.MESH
LOG2E = 1.4426950408889634
FACTOR = HS ** (-0.5)
SCALE = FACTOR * LOG2E
PARTS = (pl.ds(1, 2), pl.ds(0, 1))


def coords():
    seq = lax.axis_index("seq")
    head = lax.axis_index("head")
    x = seq // 4
    p = (seq % 4) * 8 + head
    return x, p


def device_of(x, p):
    return (x * 4 + p // 8, p % 8)


def past_six(p):
    return (p - 6) * ((p + 26) // 32)


def most_band(slot, p):
    low = (p + 6) * 24 // 63
    high = (63 - past_six(p)) * 24 // 63
    return MIN_BAND + low + slot * (high - low)


def least_band(slot, p):
    low = past_six(p) * 24 // 63
    high = (57 - p) * 24 // 63
    return MIN_BAND + low + slot * (high - low)


def head_rows(slot, p):
    head = p + slot * (HEADS - 1 - 2 * p)
    return pl.ds(pl.multiple_of(head * HS, 16), HS)


def lanes(block):
    return pl.ds(pl.multiple_of(block * BLOCK, BLOCK), BLOCK)


def flip(x):
    size = x.shape[1]
    one = (
        lax.broadcasted_iota(jnp.int32, (size, size), 0)
        == lax.broadcasted_iota(jnp.int32, (size, size), 1)
    ).astype(jnp.bfloat16)
    return lax.dot_general(
        one, x, (((1,), (1,)), ((), ())), preferred_element_type=jnp.float32
    ).astype(jnp.bfloat16)


def enter(x, p):
    barrier = pltpu.get_barrier_semaphore()

    def greet(d, carry):
        pl.semaphore_signal(
            barrier, inc=1, device_id=device_of(x, (p + d) % PLANE), device_id_type=MESH
        )
        return carry

    lax.fori_loop(1, PLANE, greet, 0)
    for d in range(1, 4):
        pl.semaphore_signal(
            barrier, inc=1, device_id=device_of((x + d) % 4, p), device_id_type=MESH
        )
    pl.semaphore_wait(barrier, PLANE - 1 + 3)


def layer_kernel(
    band_ref,
    slope_ref,
    q_hbm,
    k_hbm,
    v_hbm,
    out_hbm,
    staged,
    turned,
    kv,
    arrived,
    queries,
    acc_ref,
    mixed,
    back,
    result_ref,
    load,
    send,
    recv,
    own,
    halo_send,
    halo_recv,
    far_send,
    back_send,
    back_recv,
    store,
):
    x, p = coords()

    def load_copy(c, half):
        columns = pl.ds(half * HALF, HALF)
        return pltpu.make_async_copy(
            (q_hbm, k_hbm, v_hbm)[c].at[:, columns], staged.at[c, :, columns], load.at[c, half]
        )

    for half in (1, 0):
        for c in (1, 2, 0):
            load_copy(c, half).start()

    row = lax.broadcasted_iota(jnp.int32, (16, BLOCK), 0)
    token = lax.broadcasted_iota(jnp.int32, (16, BLOCK), 1).astype(jnp.float32)

    for slot in range(2):

        def prepare(index, carry):
            block = index - PAD
            absent = (block < -PLANE * x) | (block <= -most_band(slot, p))
            extra = jnp.where(
                row < 3,
                block.astype(jnp.float32),
                jnp.where(row < 6, token, jnp.where(row < 7, jnp.where(absent, 1.0, 0.0), 0.0)),
            )
            kv[slot, 0, HS:BLOCK, lanes(index)] = extra.astype(jnp.bfloat16)
            kv[slot, 1, HS:BLOCK, lanes(index)] = jnp.ones((16, BLOCK), jnp.bfloat16)

            @pl.when(absent)
            def _():
                for c in range(2):
                    kv[slot, c, 0:HS, lanes(index)] = jnp.zeros((HS, BLOCK), jnp.bfloat16)

            return carry

        lax.fori_loop(0, PAD + PLANE, prepare, 0)

    def turn_half(half):
        def turn(step, carry):
            for part in range(7):
                at = lanes(half * 28 + step * 7 + part)
                for c in range(3):
                    turned[c, at, :] = flip(staged[c, :, at])
            return carry

        for c in range(3):
            load_copy(c, half).wait()
        lax.fori_loop(0, 4, turn, 0)

    def message(j, slot, part, place, peer, sem):
        source = turned.at[PARTS[part], head_rows(slot, place), :]
        if part == 0:
            target = kv.at[slot, :, pl.ds(0, HS), lanes(PAD + j)]
        else:
            target = arrived.at[pl.ds(slot, 1), j]
        return pltpu.make_async_remote_copy(
            src_ref=source,
            dst_ref=target,
            send_sem=send.at[sem, slot, part],
            recv_sem=recv.at[j, slot, part],
            device_id=device_of(x, peer),
            device_id_type=MESH,
        )

    def to_peer(d, slot, part):
        peer = (p + d) % PLANE
        return message(p, slot, part, peer, peer, d)

    def from_peer(j, slot, part):
        return message(j, slot, part, 0, (p + 1) % PLANE, 0)

    def own_copy(slot, part):
        if part == 0:
            target = kv.at[slot, :, pl.ds(0, HS), lanes(PAD + p)]
        else:
            target = arrived.at[pl.ds(slot, 1), p]
        return pltpu.make_async_copy(
            turned.at[PARTS[part], head_rows(slot, p), :], target, own.at[slot, part]
        )

    def near(j, slot):
        return pltpu.make_async_remote_copy(
            src_ref=kv.at[slot, :, pl.ds(0, HS), lanes(PAD + j)],
            dst_ref=kv.at[slot, :, pl.ds(0, HS), lanes(PAD - PLANE + j)],
            send_sem=halo_send.at[j, slot],
            recv_sem=halo_recv.at[8 + j, slot],
            device_id=device_of((x + 1) % 4, p),
            device_id_type=MESH,
        )

    def far(j):
        return pltpu.make_async_remote_copy(
            src_ref=kv.at[1, :, pl.ds(0, HS), lanes(PAD + j)],
            dst_ref=kv.at[1, :, pl.ds(0, HS), lanes(PAD - 2 * PLANE + j)],
            send_sem=far_send.at[j - 24],
            recv_sem=halo_recv.at[j - 24, 1],
            device_id=device_of((x + 2) % 4, p),
            device_id_type=MESH,
        )

    def near_needed(j, slot):
        return j >= 33 - most_band(slot, p)

    def far_needed(j):
        return (j >= 25) & (j >= 65 - most_band(1, p))

    def forward(j, slot):
        @pl.when((x < 3) & near_needed(j, slot))
        def _():
            near(j, slot).start()

        if slot == 1:

            @pl.when((x < 2) & far_needed(j))
            def _():
                far(j).start()

    def start_slot(slot):
        for part in range(2):

            def start(d, carry):
                to_peer(d, slot, part).start()
                return carry

            lax.fori_loop(1, PLANE, start, 0)
            own_copy(slot, part).start()

    turn_half(1)
    enter(x, p)
    start_slot(1)
    turn_half(0)
    start_slot(0)

    def take(d, slot):
        j = (p + PLANE - d) % PLANE
        from_peer(j, slot, 0).wait_recv()
        forward(j, slot)

    for slot in (1, 0):
        own_copy(slot, 0).wait()
        forward(p, slot)

    def take_heavy(d, carry):
        take(d, 1)
        return carry

    lax.fori_loop(1, PLANE, take_heavy, 0)

    causal = lax.broadcasted_iota(jnp.int32, (ROWS, ROWS), 1) <= lax.broadcasted_iota(
        jnp.int32, (ROWS, ROWS), 0
    )

    def send_back(block, slot):
        return pltpu.make_async_remote_copy(
            src_ref=mixed.at[slot, block],
            dst_ref=back.at[head_rows(slot, p), :],
            send_sem=back_send.at[block, slot],
            recv_sem=back_recv.at[p, slot],
            device_id=device_of(x, block),
            device_id_type=MESH,
        )

    def keep_back(slot):
        return pltpu.make_async_copy(
            mixed.at[slot, p], back.at[head_rows(slot, p), :], back_recv.at[p, slot]
        )

    def got_back(j, slot):
        return pltpu.make_async_remote_copy(
            src_ref=mixed.at[slot, 0],
            dst_ref=back.at[head_rows(slot, j), :],
            send_sem=back_send.at[0, slot],
            recv_sem=back_recv.at[j, slot],
            device_id=device_of(x, (p + 1) % PLANE),
            device_id_type=MESH,
        )

    def attend(slot):
        band = band_ref[slot]

        own_copy(slot, 1).wait()

        def take_query(d, carry):
            from_peer((p + PLANE - d) % PLANE, slot, 1).wait_recv()
            return carry

        lax.fori_loop(1, PLANE, take_query, 0)
        slope = slope_ref[slot, 0:1, :] * (BLOCK / FACTOR)
        high = slope.astype(jnp.bfloat16).astype(jnp.float32)
        middle = (slope - high).astype(jnp.bfloat16).astype(jnp.float32)
        low = (slope - high - middle).astype(jnp.bfloat16).astype(jnp.float32)
        kind = row % 3
        parts = jnp.where(kind == 0, high, jnp.where(kind == 1, middle, low))
        parts = jnp.where(
            row < 3,
            parts,
            jnp.where(row < 6, parts * (1.0 / BLOCK), jnp.where(row < 7, -1e30, 0.0)),
        ).astype(jnp.bfloat16)

        def put_queries(step, carry):
            for part in range(8):
                index = step * 8 + part
                queries[lanes(index), :] = flip(
                    jnp.concatenate([arrived[slot, index], parts], axis=0)
                )
            return carry

        lax.fori_loop(0, PLANE // 8, put_queries, 0)

        def take_halo(j, carry):
            @pl.when((x > 0) & near_needed(j, slot))
            def _():
                near(j, slot).wait_recv()

            if slot == 1:

                @pl.when((x > 1) & far_needed(j))
                def _():
                    far(j).wait_recv()

            return carry

        def scores(chain, first):
            at = pl.multiple_of((first + PAD) * BLOCK, BLOCK)
            return jnp.dot(
                queries[chain * ROWS : (chain + 1) * ROWS, :],
                kv[slot, 0, :, pl.ds(at, ROWS)],
                preferred_element_type=jnp.float32,
            )

        def mix(first, weight):
            at = pl.multiple_of((first + PAD) * BLOCK, BLOCK)
            return lax.dot_general(
                weight.astype(jnp.bfloat16),
                kv[slot, 1, :, pl.ds(at, ROWS)],
                (((1,), (1,)), ((), ())),
                preferred_element_type=jnp.float32,
            )

        def sweep(tops, offset, kind):
            starts = [c * TILE + offset for c in range(CHAINS)]

            def tile(c):
                s = scores(c, starts[c])
                if kind == "first":
                    s = jnp.where(causal, s, -1e30)
                    return s, jnp.max(s, axis=1, keepdims=True)
                if kind == "edge":
                    rows = []
                    for r in range(TILE):
                        columns = []
                        for k in range(TILE):
                            far_off = jnp.where(offset + (k - r) > -band, 0.0, -1e30)
                            columns.append(
                                s[r * BLOCK : (r + 1) * BLOCK, k * BLOCK : (k + 1) * BLOCK]
                                + far_off
                            )
                        rows.append(jnp.concatenate(columns, axis=1))
                    s = jnp.concatenate(rows, axis=0)
                return s, jnp.maximum(tops[c], jnp.max(s, axis=1, keepdims=True))

            after = []
            ready = tile(0)
            for c in range(CHAINS):
                s, new = ready
                if c + 1 < CHAINS:
                    ready = tile(c + 1)
                fresh = mix(starts[c], jnp.exp2((s - new) * SCALE))
                if kind == "first":
                    acc_ref[c] = fresh
                else:
                    acc_ref[c] = acc_ref[c] * jnp.exp2((tops[c] - new) * SCALE) + fresh
                after.append(new)
            return tuple(after)

        tops = sweep(None, 0, "first")
        lax.fori_loop(0, PLANE, take_halo, 0)
        full = (least_band(slot, p) - TILE) // TILE
        total = (most_band(slot, p) + 2) // TILE

        def inner(n, tops):
            if slot == 1:
                for part in range(7):
                    d = 1 + n * 7 + part

                    @pl.when(d < PLANE)
                    def _():
                        take(d, 0)

            return sweep(tops, -TILE * (n + 1), "inner")

        tops = lax.fori_loop(0, full, inner, tops)
        lax.fori_loop(
            full, total, lambda n, tops: sweep(tops, -TILE * (n + 1), "edge"), tops
        )
        for c in range(CHAINS):
            result = (acc_ref[c, :, 0:HS] / acc_ref[c, :, HS : HS + 1]).astype(jnp.bfloat16)
            for b in range(TILE):
                block = c * TILE + b
                mixed[slot, block] = flip(result[b * BLOCK : (b + 1) * BLOCK])

        def give(d, carry):
            send_back((p + d) % PLANE, slot).start()
            return carry

        lax.fori_loop(1, PLANE, give, 0)
        keep_back(slot).start()

    attend(1)
    attend(0)

    def unturn_half(half):
        def arrive(d, carry):
            got_back((p + PLANE - d) % PLANE, half).wait_recv()
            return carry

        keep_back(half).wait()
        lax.fori_loop(1, PLANE, arrive, 0)

        def unturn(step, carry):
            for part in range(7):
                at = lanes(half * 28 + step * 7 + part)
                result_ref[:, at] = flip(back[at, :])
            return carry

        lax.fori_loop(0, 4, unturn, 0)
        columns = pl.ds(half * HALF, HALF)
        copy = pltpu.make_async_copy(
            result_ref.at[:, columns], out_hbm.at[:, columns], store.at[half]
        )
        copy.start()
        return copy

    stores = [unturn_half(1), unturn_half(0)]

    def finish(d, carry):
        for slot in range(2):

            @pl.when(d > 0)
            def _():
                for part in range(2):
                    to_peer(d, slot, part).wait_send()
                send_back((p + d) % PLANE, slot).wait_send()

            @pl.when((x < 3) & near_needed(d, slot))
            def _():
                near(d, slot).wait_send()

        @pl.when((x < 2) & far_needed(d))
        def _():
            far(d).wait_send()

        return carry

    lax.fori_loop(0, PLANE, finish, 0)
    for copy in stores:
        copy.wait()


def layer(bands, slopes, query, key, value):
    anywhere = pl.BlockSpec(memory_space=pl.ANY)
    return pl.pallas_call(
        layer_kernel,
        out_shape=jax.ShapeDtypeStruct((BLOCK, D), jnp.bfloat16),
        in_specs=[
            pl.BlockSpec(memory_space=pltpu.SMEM),
            pl.BlockSpec(memory_space=pltpu.VMEM),
            anywhere,
            anywhere,
            anywhere,
        ],
        out_specs=anywhere,
        scratch_shapes=[
            pltpu.VMEM((3, BLOCK, D), jnp.bfloat16),
            pltpu.VMEM((3, D, BLOCK), jnp.bfloat16),
            pltpu.VMEM((2, 2, BLOCK, (PAD + PLANE) * BLOCK), jnp.bfloat16),
            pltpu.VMEM((2, PLANE, HS, BLOCK), jnp.bfloat16),
            pltpu.VMEM((PLANE * BLOCK, BLOCK), jnp.bfloat16),
            pltpu.VMEM((CHAINS, ROWS, BLOCK), jnp.float32),
            pltpu.VMEM((2, PLANE, HS, BLOCK), jnp.bfloat16),
            pltpu.VMEM((D, BLOCK), jnp.bfloat16),
            pltpu.VMEM((BLOCK, D), jnp.bfloat16),
            pltpu.SemaphoreType.DMA((3, 2)),
            pltpu.SemaphoreType.DMA((PLANE, 2, 2)),
            pltpu.SemaphoreType.DMA((PLANE, 2, 2)),
            pltpu.SemaphoreType.DMA((2, 2)),
            pltpu.SemaphoreType.DMA((PLANE, 2)),
            pltpu.SemaphoreType.DMA((8 + PLANE, 2)),
            pltpu.SemaphoreType.DMA((8,)),
            pltpu.SemaphoreType.DMA((PLANE, 2)),
            pltpu.SemaphoreType.DMA((PLANE, 2)),
            pltpu.SemaphoreType.DMA((2,)),
        ],
        compiler_params=pltpu.CompilerParams(
            collective_id=0, has_side_effects=True, vmem_limit_bytes=60 << 20
        ),
        name="layer",
    )(bands, slopes, query, key, value)


def on_device(query, key, value, exponent):
    x, p = coords()
    heads = jnp.stack([p, HEADS - 1 - p])
    local = jnp.take(exponent, heads)
    bands = MIN_BAND + (local - 1) * (MAX_BAND - MIN_BAND) // (HEADS - 1)
    slopes = jnp.exp2(-12.0 * local.astype(jnp.float32) / HEADS)
    slopes = jnp.broadcast_to(slopes[:, None, None], (2, 8, BLOCK))
    return layer(bands, slopes, query, key, value)


def solution(mesh):
    return jax.shard_map(
        on_device,
        mesh=mesh,
        in_specs=(
            P(("seq", "head"), None),
            P(("seq", "head"), None),
            P(("seq", "head"), None),
            P(),
        ),
        out_specs=P(("seq", "head"), None),
        check_vma=False,
    )
```

time: 1490 us -> 161 us (0.11)
  the two profiles are of different devices: /device:TPU:21 before, /device:TPU:3 now
where the time goes in v3:
time: 161 us; the launch traced here: 160 us
  Pallas kernels  155 us (96%)
  local copies, waits for them, and re-layouts  4.72 us (3%)
    pallas_call x1, Pallas kernels, layer(): pl.pallas_call(layer_kernel, out_shape=jax.ShapeDtypeStruct((BLOCK, D), j...  155 us
    unnamed x3, local copies, waits for them, and re-layouts  3.42 us

profile of v3, /device:TPU:3, one launch (start us, length us, event | category | flops | bytes accessed | tf_op | source)
XLA Modules:
  0.0 160.4 jit_solution(11093507698058676415)
XLA Ops:
  0.0 0.0 copy-start
  0.0 0.1 fusion
  0.1 0.6 copy-done
  0.7 0.6 gather_fusion
  1.3 0.1 multiply_exponential_fusion
  1.4 0.6 fusion.1.band_ref
  2.0 0.7 broadcast_in_dim.4.slope_ref
  2.7 154.9 %layer.1 = bf16[128,7168]{1,0:T(8,128)(2,1)} custom-call(s32[2]{0:T(128)} %fusion.1.band_ref, f32[2,8,128]{2,1,0:T(8,128)} %broadcast_in_dim.4.slope_ref, bf16[128,7168]{1,0:T(8,128)(2,1)} %q_hbm.1, bf16[128,7168]{1,0:T(8,128)(2,1)} %k_hbm.1, bf16[128,7168]{1,0:T(8,128)(2,1)} %v_hbm.1), custom_call_target="tpu_custom_call" | custom-call | tf_op jit(solution)/shard_map/layer/pallas_call | solution.py:480
  157.6 2.8 %copy.6 = bf16[128,7168]{1,0:T(8,128)(2,1)} copy(bf16[128,7168]{1,0:T(8,128)(2,1)} %layer.1) | data formatting | bytes 3670016
  (1 shorter events, 0.0 us)
Async XLA Ops:
  0.0 0.7 copy-start

commit v4 on v3

--- a/solution.py
+++ b/solution.py
@@ -16,6 +16,7 @@
 PAD = 48
 TILE = 4
 ROWS = TILE * BLOCK
+STRIDE = 11
 CHAINS = PLANE // TILE
 MESH = pl.DeviceIdType.MESH
 LOG2E = 1.4426950408889634
@@ -72,7 +73,7 @@
     ).astype(jnp.bfloat16)
 
 
-def enter(x, p):
+def greet_all(x, p):
     barrier = pltpu.get_barrier_semaphore()
 
     def greet(d, carry):
@@ -86,12 +87,11 @@
         pl.semaphore_signal(
             barrier, inc=1, device_id=device_of((x + d) % 4, p), device_id_type=MESH
         )
-    pl.semaphore_wait(barrier, PLANE - 1 + 3)
+    return barrier
 
 
 def layer_kernel(
-    band_ref,
-    slope_ref,
+    exponent_ref,
     q_hbm,
     k_hbm,
     v_hbm,
@@ -128,40 +128,52 @@
         for c in (1, 2, 0):
             load_copy(c, half).start()
 
+    barrier = greet_all(x, p)
     row = lax.broadcasted_iota(jnp.int32, (16, BLOCK), 0)
     token = lax.broadcasted_iota(jnp.int32, (16, BLOCK), 1).astype(jnp.float32)
 
-    for slot in range(2):
-
-        def prepare(index, carry):
-            block = index - PAD
-            absent = (block < -PLANE * x) | (block <= -most_band(slot, p))
-            extra = jnp.where(
-                row < 3,
-                block.astype(jnp.float32),
-                jnp.where(row < 6, token, jnp.where(row < 7, jnp.where(absent, 1.0, 0.0), 0.0)),
-            )
-            kv[slot, 0, HS:BLOCK, lanes(index)] = extra.astype(jnp.bfloat16)
-            kv[slot, 1, HS:BLOCK, lanes(index)] = jnp.ones((16, BLOCK), jnp.bfloat16)
-
-            @pl.when(absent)
-            def _():
-                for c in range(2):
-                    kv[slot, c, 0:HS, lanes(index)] = jnp.zeros((HS, BLOCK), jnp.bfloat16)
-
-            return carry
-
-        lax.fori_loop(0, PAD + PLANE, prepare, 0)
-
-    def turn_half(half):
+    def absent(index, slot):
+        block = index - PAD
+        return (block < -PLANE * x) | (block <= -most_band(slot, p))
+
+    def prepare():
+        ones = jnp.ones((16, BLOCK), jnp.bfloat16)
+        zeros = jnp.zeros((HS, BLOCK), jnp.bfloat16)
+        for slot in range(2):
+
+            def extras(step, carry):
+                for part in range(8):
+                    index = step * 8 + part
+                    block = (index - PAD).astype(jnp.float32)
+                    dead = jnp.where(absent(index, slot), 1.0, 0.0)
+                    extra = jnp.where(
+                        row < 3, block, jnp.where(row < 6, token, jnp.where(row < 7, dead, 0.0))
+                    )
+                    kv[slot, 0, HS:BLOCK, lanes(index)] = extra.astype(jnp.bfloat16)
+                    kv[slot, 1, HS:BLOCK, lanes(index)] = ones
+                return carry
+
+            lax.fori_loop(0, (PAD + PLANE) // 8, extras, 0)
+
+            def clear(index, carry):
+                @pl.when(absent(index, slot))
+                def _():
+                    for c in range(2):
+                        kv[slot, c, 0:HS, lanes(index)] = zeros
+
+                return carry
+
+            lax.fori_loop(0, PAD, clear, 0)
+
+    def turn_half(half, tensors):
         def turn(step, carry):
             for part in range(7):
                 at = lanes(half * 28 + step * 7 + part)
-                for c in range(3):
+                for c in tensors:
                     turned[c, at, :] = flip(staged[c, :, at])
             return carry
 
-        for c in range(3):
+        for c in tensors:
             load_copy(c, half).wait()
         lax.fori_loop(0, 4, turn, 0)
 
@@ -181,7 +193,7 @@
         )
 
     def to_peer(d, slot, part):
-        peer = (p + d) % PLANE
+        peer = (p + STRIDE * d) % PLANE
         return message(p, slot, part, peer, peer, d)
 
     def from_peer(j, slot, part):
@@ -233,24 +245,27 @@
             def _():
                 far(j).start()
 
-    def start_slot(slot):
-        for part in range(2):
-
-            def start(d, carry):
-                to_peer(d, slot, part).start()
-                return carry
-
-            lax.fori_loop(1, PLANE, start, 0)
-            own_copy(slot, part).start()
-
-    turn_half(1)
-    enter(x, p)
-    start_slot(1)
-    turn_half(0)
-    start_slot(0)
+    def start_part(slot, part):
+        def start(d, carry):
+            to_peer(d, slot, part).start()
+            return carry
+
+        lax.fori_loop(1, PLANE, start, 0)
+        own_copy(slot, part).start()
+
+    turn_half(1, (1, 2))
+    pl.semaphore_wait(barrier, PLANE - 1 + 3)
+    start_part(1, 0)
+    turn_half(1, (0,))
+    start_part(1, 1)
+    turn_half(0, (1, 2))
+    start_part(0, 0)
+    turn_half(0, (0,))
+    start_part(0, 1)
+    prepare()
 
     def take(d, slot):
-        j = (p + PLANE - d) % PLANE
+        j = (p + STRIDE * (PLANE - d)) % PLANE
         from_peer(j, slot, 0).wait_recv()
         forward(j, slot)
 
@@ -294,16 +309,18 @@
         )
 
     def attend(slot):
-        band = band_ref[slot]
+        exponent = exponent_ref[p + slot * (HEADS - 1 - 2 * p)]
+        band = MIN_BAND + (exponent - 1) * (MAX_BAND - MIN_BAND) // (HEADS - 1)
+        power = jnp.full((1, BLOCK), exponent.astype(jnp.float32)) * (-12.0 / HEADS)
 
         own_copy(slot, 1).wait()
 
         def take_query(d, carry):
-            from_peer((p + PLANE - d) % PLANE, slot, 1).wait_recv()
+            from_peer((p + STRIDE * (PLANE - d)) % PLANE, slot, 1).wait_recv()
             return carry
 
         lax.fori_loop(1, PLANE, take_query, 0)
-        slope = slope_ref[slot, 0:1, :] * (BLOCK / FACTOR)
+        slope = jnp.exp2(power) * (BLOCK / FACTOR)
         high = slope.astype(jnp.bfloat16).astype(jnp.float32)
         middle = (slope - high).astype(jnp.bfloat16).astype(jnp.float32)
         low = (slope - high - middle).astype(jnp.bfloat16).astype(jnp.float32)
@@ -418,7 +435,7 @@
                 mixed[slot, block] = flip(result[b * BLOCK : (b + 1) * BLOCK])
 
         def give(d, carry):
-            send_back((p + d) % PLANE, slot).start()
+            send_back((p + STRIDE * d) % PLANE, slot).start()
             return carry
 
         lax.fori_loop(1, PLANE, give, 0)
@@ -429,7 +446,7 @@
 
     def unturn_half(half):
         def arrive(d, carry):
-            got_back((p + PLANE - d) % PLANE, half).wait_recv()
+            got_back((p + STRIDE * (PLANE - d)) % PLANE, half).wait_recv()
             return carry
 
         keep_back(half).wait()
@@ -449,7 +466,7 @@
         copy.start()
         return copy
 
-    stores = [unturn_half(1), unturn_half(0)]
+    stores = [unturn_half(1)]
 
     def finish(d, carry):
         for slot in range(2):
@@ -458,7 +475,6 @@
             def _():
                 for part in range(2):
                     to_peer(d, slot, part).wait_send()
-                send_back((p + d) % PLANE, slot).wait_send()
 
             @pl.when((x < 3) & near_needed(d, slot))
             def _():
@@ -471,18 +487,25 @@
         return carry
 
     lax.fori_loop(0, PLANE, finish, 0)
+    stores.append(unturn_half(0))
+
+    def finish_back(d, carry):
+        for slot in range(2):
+            send_back((p + d) % PLANE, slot).wait_send()
+        return carry
+
+    lax.fori_loop(1, PLANE, finish_back, 0)
     for copy in stores:
         copy.wait()
 
 
-def layer(bands, slopes, query, key, value):
+def layer(exponent, query, key, value):
     anywhere = pl.BlockSpec(memory_space=pl.ANY)
     return pl.pallas_call(
         layer_kernel,
         out_shape=jax.ShapeDtypeStruct((BLOCK, D), jnp.bfloat16),
         in_specs=[
             pl.BlockSpec(memory_space=pltpu.SMEM),
-            pl.BlockSpec(memory_space=pltpu.VMEM),
             anywhere,
             anywhere,
             anywhere,
@@ -513,17 +536,11 @@
             collective_id=0, has_side_effects=True, vmem_limit_bytes=60 << 20
         ),
         name="layer",
-    )(bands, slopes, query, key, value)
+    )(exponent, query, key, value)
 
 
 def on_device(query, key, value, exponent):
-    x, p = coords()
-    heads = jnp.stack([p, HEADS - 1 - p])
-    local = jnp.take(exponent, heads)
-    bands = MIN_BAND + (local - 1) * (MAX_BAND - MIN_BAND) // (HEADS - 1)
-    slopes = jnp.exp2(-12.0 * local.astype(jnp.float32) / HEADS)
-    slopes = jnp.broadcast_to(slopes[:, None, None], (2, 8, BLOCK))
-    return layer(bands, slopes, query, key, value)
+    return layer(exponent, query, key, value)
 
 
 def solution(mesh):

time: 161 us -> 142 us (0.88)
  the two profiles are of different devices: /device:TPU:3 before, /device:TPU:2 now
where the time goes in v4:
time: 142 us
  Pallas kernels  139 us (98%)
  local copies, waits for them, and re-layouts  2.85 us (2%)
    pallas_call x1, Pallas kernels, layer(): pl.pallas_call(layer_kernel, out_shape=jax.ShapeDtypeStruct((BLOCK, D), j...  139 us
    unnamed x1, local copies, waits for them, and re-layouts  2.85 us

profile of v4, /device:TPU:2, one launch (start us, length us, event | category | flops | bytes accessed | tf_op | source)
XLA Modules:
  0.0 141.5 jit_solution(8055298081867995928)
XLA Ops:
  0.0 138.7 %layer.1 = bf16[128,7168]{1,0:T(8,128)(2,1)} custom-call(s32[64]{0:T(128)} %exponent_ref.1, bf16[128,7168]{1,0:T(8,128)(2,1)} %q_hbm.1, bf16[128,7168]{1,0:T(8,128)(2,1)} %k_hbm.1, bf16[128,7168]{1,0:T(8,128)(2,1)} %v_hbm.1), custom_call_target="tpu_custom_call" | custom-call | tf_op jit(solution)/shard_map/layer/pallas_call | solution.py:504
  138.7 2.8 %copy.6 = bf16[128,7168]{1,0:T(8,128)(2,1)} copy(bf16[128,7168]{1,0:T(8,128)(2,1)} %layer.1) | data formatting | bytes 3670016

commit v5 on v4

--- a/solution.py
+++ b/solution.py
@@ -258,26 +258,26 @@
     start_part(1, 0)
     turn_half(1, (0,))
     start_part(1, 1)
+    prepare()
     turn_half(0, (1, 2))
-    start_part(0, 0)
-    turn_half(0, (0,))
-    start_part(0, 1)
-    prepare()
+    own_copy(0, 0).start()
 
     def take(d, slot):
         j = (p + STRIDE * (PLANE - d)) % PLANE
         from_peer(j, slot, 0).wait_recv()
         forward(j, slot)
 
-    for slot in (1, 0):
-        own_copy(slot, 0).wait()
-        forward(p, slot)
+    own_copy(1, 0).wait()
+    forward(p, 1)
 
     def take_heavy(d, carry):
         take(d, 1)
+        to_peer(d, 0, 0).start()
         return carry
 
     lax.fori_loop(1, PLANE, take_heavy, 0)
+    turn_half(0, (0,))
+    own_copy(0, 1).start()
 
     causal = lax.broadcasted_iota(jnp.int32, (ROWS, ROWS), 1) <= lax.broadcasted_iota(
         jnp.int32, (ROWS, ROWS), 0
@@ -317,6 +317,8 @@
 
         def take_query(d, carry):
             from_peer((p + STRIDE * (PLANE - d)) % PLANE, slot, 1).wait_recv()
+            if slot == 1:
+                to_peer(d, 0, 1).start()
             return carry
 
         lax.fori_loop(1, PLANE, take_query, 0)
@@ -342,18 +344,19 @@
 
         lax.fori_loop(0, PLANE // 8, put_queries, 0)
 
-        def take_halo(j, carry):
-            @pl.when((x > 0) & near_needed(j, slot))
-            def _():
-                near(j, slot).wait_recv()
-
-            if slot == 1:
-
-                @pl.when((x > 1) & far_needed(j))
+        def take_halo(n):
+            for part in range(TILE):
+                j = PLANE - TILE - TILE * n + part
+
+                @pl.when((x > 0) & (j >= 0) & near_needed(j, slot))
                 def _():
-                    far(j).wait_recv()
-
-            return carry
+                    near(j, slot).wait_recv()
+
+                if slot == 1:
+
+                    @pl.when((x > 1) & (j < 0) & far_needed(j + PLANE))
+                    def _():
+                        far(j + PLANE).wait_recv()
 
         def scores(chain, first):
             at = pl.multiple_of((first + PAD) * BLOCK, BLOCK)
@@ -409,7 +412,9 @@
             return tuple(after)
 
         tops = sweep(None, 0, "first")
-        lax.fori_loop(0, PLANE, take_halo, 0)
+        if slot == 1:
+            own_copy(0, 0).wait()
+            forward(p, 0)
         full = (least_band(slot, p) - TILE) // TILE
         total = (most_band(slot, p) + 2) // TILE
 
@@ -422,12 +427,15 @@
                     def _():
                         take(d, 0)
 
+            take_halo(n)
             return sweep(tops, -TILE * (n + 1), "inner")
 
+        def edge(n, tops):
+            take_halo(n)
+            return sweep(tops, -TILE * (n + 1), "edge")
+
         tops = lax.fori_loop(0, full, inner, tops)
-        lax.fori_loop(
-            full, total, lambda n, tops: sweep(tops, -TILE * (n + 1), "edge"), tops
-        )
+        lax.fori_loop(full, total, edge, tops)
         for c in range(CHAINS):
             result = (acc_ref[c, :, 0:HS] / acc_ref[c, :, HS : HS + 1]).astype(jnp.bfloat16)
             for b in range(TILE):

time: 142 us -> 134 us (0.944)
  the two profiles are of different devices: /device:TPU:2 before, /device:TPU:21 now
where the time goes in v5:
time: 134 us; the launch traced here: 133 us
  Pallas kernels  130 us (97%)
  local copies, waits for them, and re-layouts  2.85 us (2%)
    pallas_call x1, Pallas kernels, layer(): pl.pallas_call(layer_kernel, out_shape=jax.ShapeDtypeStruct((BLOCK, D), j...  130 us
    unnamed x1, local copies, waits for them, and re-layouts  2.85 us

profile of v5, /device:TPU:21, one launch (start us, length us, event | category | flops | bytes accessed | tf_op | source)
XLA Modules:
  0.0 133.1 jit_solution(13374262819252534304)
XLA Ops:
  0.0 130.3 %layer.1 = bf16[128,7168]{1,0:T(8,128)(2,1)} custom-call(s32[64]{0:T(128)} %exponent_ref.1, bf16[128,7168]{1,0:T(8,128)(2,1)} %q_hbm.1, bf16[128,7168]{1,0:T(8,128)(2,1)} %k_hbm.1, bf16[128,7168]{1,0:T(8,128)(2,1)} %v_hbm.1), custom_call_target="tpu_custom_call" | custom-call | tf_op jit(solution)/shard_map/layer/pallas_call | solution.py:512
  130.3 2.8 %copy.6 = bf16[128,7168]{1,0:T(8,128)(2,1)} copy(bf16[128,7168]{1,0:T(8,128)(2,1)} %layer.1) | data formatting | bytes 3670016

commit v6 on v5

--- a/solution.py
+++ b/solution.py
@@ -136,34 +136,28 @@
         block = index - PAD
         return (block < -PLANE * x) | (block <= -most_band(slot, p))
 
-    def prepare():
-        ones = jnp.ones((16, BLOCK), jnp.bfloat16)
-        zeros = jnp.zeros((HS, BLOCK), jnp.bfloat16)
+    def prepare(d):
         for slot in range(2):
-
-            def extras(step, carry):
-                for part in range(8):
-                    index = step * 8 + part
+            for part in range(3):
+                index = 3 * (d - 1) + part
+
+                @pl.when(index < PAD + PLANE)
+                def _():
                     block = (index - PAD).astype(jnp.float32)
                     dead = jnp.where(absent(index, slot), 1.0, 0.0)
                     extra = jnp.where(
                         row < 3, block, jnp.where(row < 6, token, jnp.where(row < 7, dead, 0.0))
                     )
                     kv[slot, 0, HS:BLOCK, lanes(index)] = extra.astype(jnp.bfloat16)
-                    kv[slot, 1, HS:BLOCK, lanes(index)] = ones
-                return carry
-
-            lax.fori_loop(0, (PAD + PLANE) // 8, extras, 0)
-
-            def clear(index, carry):
-                @pl.when(absent(index, slot))
+                    kv[slot, 1, HS:BLOCK, lanes(index)] = jnp.ones((16, BLOCK), jnp.bfloat16)
+
+            for part in range(2):
+                index = 2 * (d - 1) + part
+
+                @pl.when((index < PAD) & absent(index, slot))
                 def _():
                     for c in range(2):
-                        kv[slot, c, 0:HS, lanes(index)] = zeros
-
-                return carry
-
-            lax.fori_loop(0, PAD, clear, 0)
+                        kv[slot, c, 0:HS, lanes(index)] = jnp.zeros((HS, BLOCK), jnp.bfloat16)
 
     def turn_half(half, tensors):
         def turn(step, carry):
@@ -258,9 +252,6 @@
     start_part(1, 0)
     turn_half(1, (0,))
     start_part(1, 1)
-    prepare()
-    turn_half(0, (1, 2))
-    own_copy(0, 0).start()
 
     def take(d, slot):
         j = (p + STRIDE * (PLANE - d)) % PLANE
@@ -270,12 +261,23 @@
     own_copy(1, 0).wait()
     forward(p, 1)
 
+    for c in (1, 2):
+        load_copy(c, 0).wait()
+
     def take_heavy(d, carry):
         take(d, 1)
-        to_peer(d, 0, 0).start()
+
+        @pl.when(d <= 28)
+        def _():
+            at = lanes(d - 1)
+            for c in (1, 2):
+                turned[c, at, :] = flip(staged[c, :, at])
+
+        prepare(d)
         return carry
 
     lax.fori_loop(1, PLANE, take_heavy, 0)
+    own_copy(0, 0).start()
     turn_half(0, (0,))
     own_copy(0, 1).start()
 
@@ -318,10 +320,17 @@
         def take_query(d, carry):
             from_peer((p + STRIDE * (PLANE - d)) % PLANE, slot, 1).wait_recv()
             if slot == 1:
+                to_peer(d, 0, 0).start()
+            return carry
+
+        lax.fori_loop(1, PLANE, take_query, 0)
+        if slot == 1:
+
+            def ask(d, carry):
                 to_peer(d, 0, 1).start()
-            return carry
-
-        lax.fori_loop(1, PLANE, take_query, 0)
+                return carry
+
+            lax.fori_loop(1, PLANE, ask, 0)
         slope = jnp.exp2(power) * (BLOCK / FACTOR)
         high = slope.astype(jnp.bfloat16).astype(jnp.float32)
         middle = (slope - high).astype(jnp.bfloat16).astype(jnp.float32)

time: 134 us -> 133 us (level)
  no operation moved by 1% of the time
where the time goes in v6:
time: 133 us; the launch traced here: 132 us
  Pallas kernels  130 us (98%)
  local copies, waits for them, and re-layouts  2.85 us (2%)
    pallas_call x1, Pallas kernels, layer(): pl.pallas_call(layer_kernel, out_shape=jax.ShapeDtypeStruct((BLOCK, D), j...  130 us
    unnamed x1, local copies, waits for them, and re-layouts  2.85 us

profile of v6, /device:TPU:21, one launch (start us, length us, event | category | flops | bytes accessed | tf_op | source)
XLA Modules:
  0.0 132.5 jit_solution(15268206939750827779)
XLA Ops:
  0.0 129.6 %layer.1 = bf16[128,7168]{1,0:T(8,128)(2,1)} custom-call(s32[64]{0:T(128)} %exponent_ref.1, bf16[128,7168]{1,0:T(8,128)(2,1)} %q_hbm.1, bf16[128,7168]{1,0:T(8,128)(2,1)} %k_hbm.1, bf16[128,7168]{1,0:T(8,128)(2,1)} %v_hbm.1), custom_call_target="tpu_custom_call" | custom-call | tf_op jit(solution)/shard_map/layer/pallas_call | solution.py:521
  129.6 2.8 %copy.6 = bf16[128,7168]{1,0:T(8,128)(2,1)} copy(bf16[128,7168]{1,0:T(8,128)(2,1)} %layer.1) | data formatting | bytes 3670016
